TPU v7x, 32 devices: a whole 2x2x4 slice. The times are simulated.
32 devices in a mesh: dp: 8 (over z, y), pair: 4 (over x, core).
Axes of the slice: x: 2, y: 2, z: 4, core: 2. Of those that a mesh axis runs over, the one named last changes fastest.
Arguments:
- token_owner: int32 [64, 512, 1], P(('dp', 'pair')), may hold values from 0 to 7; in each aligned block of 1024 rows (0 to 1023, 1024 to 2047, ..., all dimensions but the last counted through in order) at most 256 rows name the same one
- token_row: int32 [64, 512], P(('dp', 'pair')), may hold values from 0 to 4015
- lengths: int32 [64], P(('dp', 'pair')), may hold values from 1 to 512, 20480 in all
- positives: int32 [64], replicated, may hold values from 0 to 63
- negatives: int32 [64, 7], replicated, may hold values from 0 to 63
- neg_counts: int32 [64], replicated, may hold values from 1 to 7
- embed_table: float32 [32128, 768], P('dp'), may hold values from -6 to 6
- embed_first: float32 [32128, 768], P('dp'), may hold values from -2.861023e-06 to 2.861023e-06
- embed_second: float32 [32128, 768], P('dp'), may hold values from 1.968368e-14 to 7.873472e-14
- qkv_weight: float32 [768, 2304], P(('dp', 'pair')), may hold values from -0.21875 to 0.21875
- qkv_first: float32 [768, 2304], P(('dp', 'pair')), may hold values from -5.722046e-06 to 5.722046e-06
- qkv_second: float32 [768, 2304], P(('dp', 'pair')), may hold values from 7.873472e-14 to 3.1493888e-13
- out_weight: float32 [768, 768], P(('dp', 'pair')), may hold values from -1.75 to 1.75
- out_first: float32 [768, 768], P(('dp', 'pair')), may hold values from -5.722046e-06 to 5.722046e-06
- out_second: float32 [768, 768], P(('dp', 'pair')), may hold values from 7.873472e-14 to 3.1493888e-13
- in_weight: float32 [768, 3072], P(('dp', 'pair')), may hold values from -0.21875 to 0.21875
- in_first: float32 [768, 3072], P(('dp', 'pair')), may hold values from -5.722046e-06 to 5.722046e-06
- in_second: float32 [768, 3072], P(('dp', 'pair')), may hold values from 7.873472e-14 to 3.1493888e-13
- down_weight: float32 [3072, 768], P(('dp', 'pair')), may hold values from -0.109375 to 0.109375
- down_first: float32 [3072, 768], P(('dp', 'pair')), may hold values from -5.722046e-06 to 5.722046e-06
- down_second: float32 [3072, 768], P(('dp', 'pair')), may hold values from 7.873472e-14 to 3.1493888e-13
- norm_gains: float32 [3, 768], replicated, may hold values from 0.5 to 1.5
- gains_first: float32 [3, 768], replicated, may hold values from -2.2888184e-05 to 2.2888184e-05
- gains_second: float32 [3, 768], replicated, may hold values from 1.2597555e-12 to 5.039022e-12
- position_bias: float32 [32, 12], replicated, may hold values from -3 to 3
- bias_first: float32 [32, 12], replicated, may hold values from -2.2888184e-05 to 2.2888184e-05
- bias_second: float32 [32, 12], replicated, may hold values from 1.2597555e-12 to 5.039022e-12
Outputs:
- loss_value: float32 [], replicated
- clip_norm: float32 [], replicated
- embed_new: float32 [32128, 768], P('dp')
- embed_first_new: float32 [32128, 768], P('dp')
- embed_second_new: float32 [32128, 768], P('dp')
- qkv_new: float32 [768, 2304], P(('dp', 'pair'))
- qkv_first_new: float32 [768, 2304], P(('dp', 'pair'))
- qkv_second_new: float32 [768, 2304], P(('dp', 'pair'))
- out_new: float32 [768, 768], P(('dp', 'pair'))
- out_first_new: float32 [768, 768], P(('dp', 'pair'))
- out_second_new: float32 [768, 768], P(('dp', 'pair'))
- in_new: float32 [768, 3072], P(('dp', 'pair'))
- in_first_new: float32 [768, 3072], P(('dp', 'pair'))
- in_second_new: float32 [768, 3072], P(('dp', 'pair'))
- down_new: float32 [3072, 768], P(('dp', 'pair'))
- down_first_new: float32 [3072, 768], P(('dp', 'pair'))
- down_second_new: float32 [3072, 768], P(('dp', 'pair'))
- gains_new: float32 [3, 768], replicated
- gains_first_new: float32 [3, 768], replicated
- gains_second_new: float32 [3, 768], replicated
- bias_new: float32 [32, 12], replicated
- bias_first_new: float32 [32, 12], replicated
- bias_second_new: float32 [32, 12], replicated
Inputs may be any that keep to these rules, and one draw needn't show every extreme that they name: `token_owner`: within each aligned block of 1024 tokens, no owner is named by more than 256 tokens, a bound that some block reaches. The lengths add up to 20480, and the longest is exactly 512.
All inputs are finite; a program needn't handle non-finite values. No bound on the sum of `lengths` on one device may be relied on, other than what follows from the above.
Results may differ from a plain program's by a relative error of at most 0.012.
The roundings to bfloat16 on the way count: a program that leaves them out, or rounds other values in their place, can miss the bound.
Values may be sent and summed in bfloat16 or wider, within the bound.
A program may use at most 256 MiB of HBM per device.

v0:
```python
import functools
import math

import jax
import jax.numpy as jnp
import numpy as np
from jax import lax
from jax.experimental import pallas as pl
from jax.experimental.pallas import tpu as pltpu
from jax.sharding import PartitionSpec as P

REACH = 128
STEP = 5


rms_eps = 1e-06
clip_limit = 0.05
margin = 1.0
sim_scale = 20.0
beta_one = 0.9
beta_two = 0.999
adam_eps = 1e-08
HIGHEST = lax.Precision.HIGHEST
CONTRACT_ROWS = (((0,), (0,)), ((), ()))
CONTRACT_COLS = (((1,), (1,)), ((), ()))


def bucket_of(offsets, bucket_count, reach_limit):
    half_count = bucket_count // 2
    exact_count = half_count // 2
    sign_base = jnp.where(offsets > 0, half_count, 0).astype(jnp.int32)
    distance = jnp.abs(offsets)
    far_bucket = jnp.full(offsets.shape, exact_count, jnp.int32)
    for level_index in range(1, half_count - exact_count):
        threshold = int(
            math.ceil(
                exact_count
                * (reach_limit / exact_count) ** (level_index / (half_count - exact_count))
                - 1e-09
            )
        )
        far_bucket = far_bucket + (distance >= threshold).astype(jnp.int32)
    return sign_base + jnp.where(distance < exact_count, distance, far_bucket)


def rms_forward(values, gain):
    inverse = lax.rsqrt(jnp.mean(values * values, axis=-1, keepdims=True) + rms_eps)
    return (values * inverse * gain, inverse)


def rms_backward(values, inverse, gain, upstream):
    scaled = upstream * gain
    normed = values * inverse
    grad_values = inverse * (scaled - normed * jnp.mean(scaled * normed, axis=-1, keepdims=True))
    return (grad_values, jnp.sum(upstream * normed, axis=0))


def margin_loss(pooled, positives, negatives, neg_counts):
    unit = pooled * lax.rsqrt(jnp.sum(pooled * pooled, axis=-1, keepdims=True) + 1e-06)
    similar = sim_scale * jnp.dot(unit, unit.T, precision=HIGHEST)
    chosen = jnp.take_along_axis(similar, positives[:, None], axis=1)
    against = jnp.take_along_axis(similar, negatives, axis=1)
    live_slots = jnp.arange(negatives.shape[1])[None, :] < neg_counts[:, None]
    terms = jnp.where(live_slots, jax.nn.softplus(margin - chosen + against), 0.0)
    return jnp.mean(jnp.sum(terms, axis=1) / neg_counts.astype(jnp.float32))


def doc_scores(query_heads, key_heads, bias_full, live_keys):
    scores = (
        jnp.einsum("qhd,khd->hqk", query_heads, key_heads, preferred_element_type=jnp.float32)
        * 0.125
        + bias_full
    )
    return jnp.where(live_keys[None, None, :], scores, -1000000000.0)


def attend_forward(query_heads, key_heads, value_heads, bias_full, live_keys):
    scores = doc_scores(query_heads, key_heads, bias_full, live_keys)
    highest = jnp.max(scores, axis=-1, keepdims=True)
    weights = jnp.exp(scores - highest)
    totals = jnp.sum(weights, axis=-1, keepdims=True)
    probabilities = (weights / totals).astype(jnp.bfloat16)
    attended = jnp.einsum(
        "hqk,khd->qhd", probabilities, value_heads, preferred_element_type=jnp.float32
    )
    return (attended, highest + jnp.log(totals))


def attend_backward(
    query_heads, key_heads, value_heads, bias_full, live_keys, logsum, grad_attended
):
    probabilities = jnp.exp(doc_scores(query_heads, key_heads, bias_full, live_keys) - logsum)
    grad_value = jnp.einsum(
        "hqk,qhd->khd",
        probabilities.astype(jnp.bfloat16),
        grad_attended,
        preferred_element_type=jnp.float32,
    )
    grad_prob = jnp.einsum(
        "qhd,khd->hqk", grad_attended, value_heads, preferred_element_type=jnp.float32
    )
    grad_score = probabilities * (
        grad_prob - jnp.sum(probabilities * grad_prob, axis=-1, keepdims=True)
    )
    grad_low = grad_score.astype(jnp.bfloat16)
    grad_query = (
        jnp.einsum("hqk,khd->qhd", grad_low, key_heads, preferred_element_type=jnp.float32) * 0.125
    )
    grad_key = (
        jnp.einsum("hqk,qhd->khd", grad_low, query_heads, preferred_element_type=jnp.float32)
        * 0.125
    )
    return (grad_query, grad_key, grad_value, grad_low)


def adam_step(weight, first, second, grad, rate, shrink):
    first_new = beta_one * first + (1.0 - beta_one) * grad
    second_new = beta_two * second + (1.0 - beta_two) * grad * grad
    first_hat = first_new / (1.0 - beta_one**STEP)
    second_hat = second_new / (1.0 - beta_two**STEP)
    weight_new = weight - rate * (first_hat / (jnp.sqrt(second_hat) + adam_eps) + shrink * weight)
    return (weight_new, first_new, second_new)


MESH = pl.DeviceIdType.MESH
VMEM_LIMIT = 64 * 1024 * 1024 - 65536
ANY = pl.BlockSpec(memory_space=pl.ANY)
VM = pl.BlockSpec(memory_space=pltpu.VMEM)


def place(index, n_pair):
    return {"dp": index // n_pair, "pair": lax.rem(index, n_pair)}


def remote(src, dst, send, recv, target):
    return pltpu.make_async_remote_copy(
        src, dst, send, recv, device_id=target, device_id_type=MESH
    )


def greet(targets):
    sem = pltpu.get_barrier_semaphore()
    for target in targets:
        pl.semaphore_signal(sem, inc=1, device_id=target, device_id_type=MESH)
    pl.semaphore_wait(sem, len(targets))


def my_index(n_pair):
    return lax.axis_index("dp") * n_pair + lax.axis_index("pair")


def bit_order(n_dp, n_pair, color):
    dp_bits, pair_bits = (n_dp - 1).bit_length(), (n_pair - 1).bit_length()
    high = list(reversed(range(pair_bits + 1, pair_bits + dp_bits))) + [pair_bits]
    side = list(reversed(range(1, pair_bits)))
    return high + side if color == 0 else side + high


def offset(order, position):
    return sum(((position >> step) & 1) << bit for step, bit in enumerate(order))


class Rounds:
    def __init__(self, n_dp, n_pair, dp_sem, pair_sem, own_sem):
        self.n_dp, self.n_pair = n_dp, n_pair
        self.dp_sem, self.pair_sem, self.own_sem = dp_sem, pair_sem, own_sem
        self.dp, self.pair = lax.axis_index("dp"), lax.axis_index("pair")
        sem = pltpu.get_barrier_semaphore()
        targets = [{"dp": self.dp ^ j, "pair": self.pair} for j in range(1, n_dp)]
        targets += [{"dp": self.dp, "pair": self.pair ^ j} for j in range(1, n_pair)]
        for target in targets:
            pl.semaphore_signal(sem, inc=1, device_id=target, device_id_type=MESH)
        self.entered = lambda: pl.semaphore_wait(sem, len(targets))

    def over_dp(self, block, by_dp):
        def copy(j, slot):
            target = {"dp": self.dp ^ j, "pair": self.pair}
            return remote(block, by_dp.at[slot], self.dp_sem.at[0, j], self.dp_sem.at[1, j], target)

        self.exchange(block, by_dp, self.dp, self.n_dp, copy)

    def over_pair(self, block, by_pair):
        def copy(j, slot):
            target = {"dp": self.dp, "pair": self.pair ^ j}
            return remote(
                block, by_pair.at[slot], self.pair_sem.at[0, j], self.pair_sem.at[1, j], target
            )

        self.exchange(block, by_pair, self.pair, self.n_pair, copy)

    def exchange(self, block, places, me, size, copy):
        own = pltpu.make_async_copy(block, places.at[me], self.own_sem)
        own.start()
        for j in reversed(range(1, size)):
            copy(j, me).start()
        own.wait()
        for j in range(1, size):
            copy(j, me ^ j).wait_recv()
        for j in range(1, size):
            copy(j, me).wait_send()


def round_sems(n_dp, n_pair):
    sem = pltpu.SemaphoreType.DMA
    return [sem((2, n_dp)), sem((2, n_pair)), sem]


def loss_kernel(
    n_dp, n_pair, x_ref, pos_ref, neg_ref, count_ref, loss_ref, grad_ref, by_dp, by_pair, unit, *sems
):
    rounds = Rounds(n_dp, n_pair, *sems)
    rounds.entered()
    rounds.over_dp(x_ref, by_dp)
    rounds.over_pair(by_dp, by_pair)
    docs, width = x_ref.shape
    total = n_dp * n_pair * docs
    for d in range(n_dp):
        for p in range(n_pair):
            base = (d * n_pair + p) * docs
            unit[base : base + docs] = by_pair[p, d]
    pooled = unit[...]
    inverse = lax.rsqrt(jnp.sum(pooled * pooled, axis=1, keepdims=True) + 1e-06)
    units = pooled * inverse
    similar = 20.0 * lax.dot_general(
        units, units, NT, precision=HIGHEST, preferred_element_type=jnp.float32
    )
    partner = lax.broadcasted_iota(jnp.int32, (total, total), 0)
    is_pos = partner == pos_ref[...]
    chosen = jnp.sum(jnp.where(is_pos, similar, 0.0), axis=0, keepdims=True)
    counts = count_ref[...]
    weight = 1.0 / (counts.astype(jnp.float32) * total)
    losses = jnp.zeros((1, total), jnp.float32)
    slopes = jnp.zeros((1, total), jnp.float32)
    grad_similar = jnp.zeros((total, total), jnp.float32)
    for slot in range(neg_ref.shape[0]):
        is_neg = partner == neg_ref[slot : slot + 1, :]
        against = jnp.sum(jnp.where(is_neg, similar, 0.0), axis=0, keepdims=True)
        value = margin - chosen + against
        used = slot < counts
        soft = jnp.maximum(value, 0.0) + jnp.log1p(jnp.exp(-jnp.abs(value)))
        losses = losses + jnp.where(used, soft, 0.0)
        slope = jnp.where(used, weight / (1.0 + jnp.exp(-value)), 0.0)
        grad_similar = grad_similar + jnp.where(is_neg, slope, 0.0)
        slopes = slopes + slope
    grad_similar = grad_similar - jnp.where(is_pos, slopes, 0.0)
    loss_ref[...] = jnp.sum(losses * weight, axis=1, keepdims=True)
    grad_units = sim_scale * (
        jnp.dot(grad_similar, units, precision=HIGHEST, preferred_element_type=jnp.float32)
        + lax.dot_general(
            grad_similar, units, TN, precision=HIGHEST, preferred_element_type=jnp.float32
        )
    )
    inner = jnp.sum(grad_units * units, axis=1, keepdims=True)
    unit[...] = inverse * (grad_units - units * inner)
    for d in range(n_dp):
        for p in range(n_pair):
            base = (d * n_pair + p) * docs

            @pl.when((rounds.dp == d) & (rounds.pair == p))
            def _():
                grad_ref[...] = unit[base : base + docs]


def pooled_loss(pooled, positives, negatives, counts, cid):
    n_dp, n_pair = lax.axis_size("dp"), lax.axis_size("pair")
    docs, width = pooled.shape
    return pl.pallas_call(
        functools.partial(loss_kernel, n_dp, n_pair),
        out_shape=[
            jax.ShapeDtypeStruct((1, 1), jnp.float32),
            jax.ShapeDtypeStruct(pooled.shape, jnp.float32),
        ],
        in_specs=[VM] * 4,
        out_specs=[VM] * 2,
        scratch_shapes=[
            pltpu.VMEM((n_dp, docs, width), jnp.float32),
            pltpu.VMEM((n_pair, n_dp, docs, width), jnp.float32),
            pltpu.VMEM((n_dp * n_pair * docs, width), jnp.float32),
        ]
        + round_sems(n_dp, n_pair),
        compiler_params=pltpu.CompilerParams(collective_id=cid, has_side_effects=True),
        name="pooled_loss",
    )(pooled, positives.reshape(1, -1), negatives.T, counts.reshape(1, -1))


NT = (((1,), (1,)), ((), ()))
TN = (((0,), (0,)), ((), ()))

def band(w_ref, row, h, table, seq):
    tiles = seq // 128
    for d in range(1 - tiles, tiles):
        low = seq + 128 * d - 128
        x = jnp.broadcast_to(w_ref[pl.ds(row, 1), low : low + 256], (128, 256))
        tile = pltpu.roll(x, 0, 1, stride=1, stride_axis=0)[:, 128:]
        for a in range(tiles):
            if 0 <= a + d < tiles:
                table[h, a * 128 : a * 128 + 128, (a + d) * 128 : (a + d) * 128 + 128] = tile

def forward_kernel(len_ref, q_ref, k_ref, v_ref, w_ref, o_ref, table):
    seq = q_ref.shape[0]
    doc = pl.program_id(1)
    @pl.when(doc == 0)
    def _():
        for h in range(2):
            band(w_ref, 2 * pl.program_id(0) + h, h, table, seq)
    length = len_ref[doc]
    lane = lax.broadcasted_iota(jnp.int32, (seq, 128), 1)
    column = lax.broadcasted_iota(jnp.int32, (1, seq), 1)
    q = q_ref[...] * jnp.bfloat16(0.125)
    k = k_ref[...]
    v = v_ref[...]
    got = []
    for h in range(2):
        mine = (lane < 64) == (h == 0)
        s = lax.dot_general(jnp.where(mine, q, 0), k, NT, preferred_element_type=jnp.float32)
        s = jnp.where(column < length, s + table[h], -1000000000.0)
        e = jnp.exp(s - jnp.max(s, axis=1, keepdims=True))
        p = (e * (1.0 / jnp.sum(e, axis=1, keepdims=True))).astype(jnp.bfloat16)
        got.append(jnp.dot(p, v, preferred_element_type=jnp.float32))
    o_ref[...] = jnp.where(lane < 64, got[0], got[1]).astype(o_ref.dtype)

def attention(lengths, qkv, w, seq):
    tokens = qkv.shape[0]
    pairs = w.shape[0] // 2
    docs = tokens // seq
    spec = lambda base: pl.BlockSpec((seq, 128), lambda h, d, *_: (d, base + h))
    return pl.pallas_call(
        forward_kernel,
        grid_spec=pltpu.PrefetchScalarGridSpec(
            num_scalar_prefetch=1, grid=(pairs, docs),
            in_specs=[spec(0), spec(pairs), spec(2 * pairs), pl.BlockSpec(w.shape, lambda h, d, *_: (0, 0))],
            out_specs=spec(0),
            scratch_shapes=[pltpu.VMEM((2, seq, seq), jnp.float32)]),
        out_shape=jax.ShapeDtypeStruct((tokens, pairs * 128), jnp.bfloat16),
        compiler_params=pltpu.CompilerParams(dimension_semantics=("arbitrary", "arbitrary"), vmem_limit_bytes=50 * 1024 * 1024),
        name="attention",
    )(lengths, qkv, qkv, qkv, w)

def bucket_hits(offsets, buckets):
    half = buckets // 2
    exact = half // 2
    distance = np.abs(offsets)
    far = np.full(offsets.shape, exact)
    for level in range(1, half - exact):
        limit = math.ceil(exact * (REACH / exact) ** (level / (half - exact)) - 1e-09)
        far = far + (distance >= limit)
    bucket = np.where(offsets > 0, half, 0) + np.where(distance < exact, distance, far)
    return (bucket[:, None] == np.arange(buckets)[None, :]).astype(np.float32)


def bias_rows(bias, seq, sign):
    hits = bucket_hits(sign * (np.arange(2 * seq) - seq), bias.shape[1])
    return jnp.dot(bias, hits.T, precision=HIGHEST)


def bias_gradient(sums, seq, buckets):
    heads, width = sums.shape[0] * 2, sums.shape[2] * sums.shape[3]
    j = np.arange(256)
    offsets = [np.where(j < 255, 128 * d + 127 - j, 0) for d in (-1, 0, 1)]
    offsets += [np.full((256,), 1 - seq), np.full((256,), seq - 1)]
    hits = bucket_hits(np.concatenate(offsets), buckets)
    hits = np.concatenate([hits, np.zeros((width - hits.shape[0], buckets), np.float32)])
    return jnp.dot(sums.reshape(heads, width), hits, precision=HIGHEST)


def weight_pieces(widths):
    cut = widths[3] * 2 // 3 // 128 * 128
    return [
        (0, 0, widths[0], 1),
        (2, 0, widths[2], 0),
        (1, 0, widths[1], 0),
        (3, 0, cut, 0),
        (3, cut, widths[3], 1),
    ]


def early_pieces(width):
    cut = width * 2 // 3 // 128 * 128
    return [(0, 0, cut, 0), (0, cut, width, 1)]


def late_pieces(widths):
    return [(2, 0, widths[2], 0), (0, 0, widths[0], 1), (1, 0, widths[1], 1)]


NN = (((1,), (0,)), ((), ()))


def stage(r):
    return (0, 1) if r == 0 else (1 << (r - 1), 1 << (r - 1))


class Gather:
    def __init__(self, n_dp, n_pair, pieces, outs, bufs, sems):
        self.n_pair, self.pieces, self.outs, self.bufs = n_pair, pieces, outs, bufs
        self.hop_sem, self.side_sem, self.core_sem, self.out_sem = sems
        self.me = my_index(n_pair)
        self.hops = (n_dp * n_pair - 1).bit_length() - 2
        self.orders = [bit_order(n_dp, n_pair, piece[3]) for piece in pieces]
        self.count = len(pieces)

    def send(self, a, lo, count, to, sem, which, bit):
        return remote(
            self.bufs[a].at[pl.ds(lo, count)],
            self.bufs[a].at[pl.ds(to, count)],
            sem.at[0, a, which],
            sem.at[1, a, which],
            place(self.me ^ (1 << bit), self.n_pair),
        )

    def hop(self, a, r):
        return self.send(a, 0, 1 << r, 1 << r, self.hop_sem, r, self.orders[a][r])

    def side(self, a, r):
        lo, count = stage(r)
        return self.send(a, lo, count, (1 << self.hops) + lo, self.side_sem, r, self.orders[a][self.hops])

    def core(self, a, r, sided):
        lo, count = stage(r)
        lo = lo + (sided << self.hops)
        return self.send(
            a, lo, count, (2 << self.hops) + lo, self.core_sem, 2 * r + sided, 0
        )

    def write_out(self, a, lo, count):
        which, low, high, _ = self.pieces[a]
        for p in range(lo, lo + count):
            block = self.me ^ offset(self.orders[a] + [0], p)
            pltpu.make_async_copy(
                self.bufs[a].at[p], self.outs[which].at[block, :, pl.ds(low, high - low)], self.out_sem.at[a]
            ).start()

    def held(self, r):
        lo, count = stage(r)
        for a in range(self.count):
            if r:
                self.hop(a, r - 1).wait_recv()
            if r < self.hops:
                self.hop(a, r).start()
            self.side(a, r).start()
            self.core(a, r, 0).start()
        for a in range(self.count):
            self.write_out(a, lo, count)

    def sided(self, r):
        lo, count = stage(r)
        for a in range(self.count):
            self.side(a, r).wait_recv()
            self.core(a, r, 1).start()
            self.write_out(a, (1 << self.hops) + lo, count)

    def cored(self, r):
        lo, count = stage(r)
        for sided in (0, 1):
            for a in range(self.count):
                self.core(a, r, sided).wait_recv()
                self.write_out(a, (2 << self.hops) + (sided << self.hops) + lo, count)

    def finish(self):
        for a in range(self.count):
            for r in range(self.hops):
                self.hop(a, r).wait_send()
            for r in range(self.hops + 1):
                self.side(a, r).wait_send()
                self.core(a, r, 0).wait_send()
                self.core(a, r, 1).wait_send()
            pltpu.make_async_copy(self.bufs[a], self.bufs[a], self.out_sem.at[a]).wait()


def triangle(size):
    rows = lax.broadcasted_iota(jnp.int32, (size, size), 0)
    columns = lax.broadcasted_iota(jnp.int32, (size, size), 1)
    return jnp.where(rows < columns, 1.0, 0.0).astype(jnp.bfloat16)


def digits(numbers):
    high = numbers // 64
    row = lax.broadcasted_iota(jnp.int32, (8, numbers.shape[1]), 0)
    both = jnp.where(row == 0, high, jnp.where(row == 1, numbers - 64 * high, 0))
    return both.astype(jnp.float32).astype(jnp.bfloat16)


def upright(pairs):
    row = lax.broadcasted_iota(jnp.int32, (8, 128), 0)
    value = jnp.where(row == 0, 64.0, jnp.where(row == 1, 1.0, 0.0)).astype(jnp.bfloat16)
    return lax.dot_general(pairs, value, TN, preferred_element_type=jnp.float32)


def hits_by_lane(numbers, width, base):
    lane = lax.broadcasted_iota(jnp.int32, (1, 128), 1).astype(jnp.float32) + base
    tiles = [
        jnp.where(numbers == lane + 128.0 * tile, 1.0, 0.0).astype(jnp.bfloat16)
        for tile in range(width // 128)
    ]
    return jnp.concatenate(tiles, axis=1)


def front_kernel(n_dp, n_pair, pieces, n_in, *refs):
    k = len(pieces)
    owner_ref, row_ref, table_ref = refs[:3]
    shards = refs[3 : 3 + n_in]
    emb_ref, key_ref, asked_ref = refs[3 + n_in : 6 + n_in]
    outs = refs[6 + n_in : 6 + 2 * n_in]
    rest = refs[6 + 2 * n_in :]
    bufs, rest = rest[:k], rest[k:]
    wide, table, ask_out, ask_in, rows_out, rows_in, total = rest[:7]
    table_sem, ask_sem, row_sem, *sems = rest[7:]
    dp, pair = lax.axis_index("dp"), lax.axis_index("pair")
    weights = Gather(n_dp, n_pair, pieces, outs, bufs, sems)
    tokens = owner_ref.shape[1]
    cap = ask_out.shape[2]
    table_rows = table_ref.shape[0]
    load = pltpu.make_async_copy(table_ref, wide, table_sem)
    load.start()
    peers = [{"dp": dp ^ j, "pair": pair} for j in range(1, n_dp)]
    sem = pltpu.get_barrier_semaphore()
    mates = [{"dp": dp, "pair": pair ^ j} for j in (1, 2)]
    for target in peers + mates:
        pl.semaphore_signal(sem, inc=1, device_id=target, device_id_type=MESH)
    for a, (which, low, high, _) in enumerate(pieces):
        bufs[a][0] = shards[which][:, low:high].astype(jnp.bfloat16)
    pl.semaphore_wait(sem, n_dp + 1)
    weights.held(0)

    owner = owner_ref[...]
    by_owner = lax.broadcasted_iota(jnp.int32, (n_dp, tokens), 0) == owner
    ranks = jnp.dot(
        jnp.where(by_owner, 1.0, 0.0).astype(jnp.bfloat16),
        triangle(tokens),
        preferred_element_type=jnp.float32,
    )
    rank = jnp.sum(jnp.where(by_owner, ranks, 0.0), axis=0, keepdims=True)
    key = owner * cap + rank.astype(jnp.int32)
    key_ref[...] = key
    wanted = digits(row_ref[...])

    def peer(j):
        return {"dp": dp ^ j, "pair": pair}

    def ask(j):
        return remote(ask_out.at[j], ask_in.at[j], ask_sem.at[0, j], ask_sem.at[1, j], peer(j))

    def reply(j):
        return remote(rows_out.at[j], rows_in.at[j], row_sem.at[0, j], row_sem.at[1, j], peer(j))

    def loop(first, last, body):
        def turn(t, carry):
            body(n_dp - 1 - t)
            return carry

        lax.fori_loop(first, last, turn, 0)

    def request(j):
        slot = lax.broadcasted_iota(jnp.int32, (cap, tokens), 0) + (dp ^ j) * cap
        chosen = jnp.where(slot == key, 1.0, 0.0).astype(jnp.bfloat16)
        ask_out[j] = lax.dot_general(wanted, chosen, NT, preferred_element_type=jnp.float32)

        @pl.when(j > 0)
        def _():
            ask(j).start()

    loop(0, n_dp, request)
    ask_in[0] = ask_out[0]
    weights.held(1)
    load.wait()

    def narrow(i, carry):
        part = pl.ds(pl.multiple_of(i * 16, 16), 16)
        table[part] = wide[part].astype(jnp.bfloat16)
        return carry

    lax.fori_loop(0, table_rows // 16, narrow, 0)
    if table.shape[0] > table_rows:
        table[table_rows:] = jnp.zeros((table.shape[0] - table_rows, table.shape[1]), jnp.bfloat16)

    def answer(j):
        @pl.when(j > 0)
        def _():
            ask(j).wait_recv()

        asked = ask_in[j]
        hit = hits_by_lane(upright(asked.astype(jnp.bfloat16)), table.shape[0], 0.0)
        got = jnp.dot(hit, table[...], preferred_element_type=jnp.float32)
        rows_out[j] = got.astype(jnp.bfloat16)
        asked_ref[j] = (64.0 * asked[0:1] + asked[1:2]).astype(jnp.int32)

        @pl.when(j > 0)
        def _():
            reply(j).start()

    early = n_dp // 4 + 1
    loop(0, early, answer)
    weights.held(2)
    weights.sided(0)
    loop(early, n_dp, answer)
    rows_in[0] = rows_out[0]
    weights.sided(1)
    upright_key = upright(digits(key))

    total[...] = jnp.zeros_like(total)

    def seat(j):
        @pl.when(j > 0)
        def _():
            reply(j).wait_recv()

        place_hit = hits_by_lane(upright_key, cap, ((dp ^ j) * cap).astype(jnp.float32))
        total[...] += jnp.dot(place_hit, rows_in[j], preferred_element_type=jnp.float32)

    weights.cored(0)
    for r in range(3, weights.hops + 1):
        weights.held(r)
        weights.sided(r - 1)
        weights.cored(r - 2)
    loop(0, n_dp, seat)
    emb_ref[...] = total[...].astype(jnp.bfloat16)
    weights.sided(weights.hops)
    for r in (weights.hops - 1, weights.hops):
        weights.cored(r)
    for j in range(1, n_dp):
        ask(j).wait_send()
        reply(j).wait_send()
    weights.finish()


def front(owner, row, table, shards, pieces, cap, n_dp, n_pair, cid):
    n, k = n_dp * n_pair, len(pieces)
    hops = (n - 1).bit_length() - 2
    tokens = owner.shape[1]
    table_rows, width = table.shape
    padded = -(-table_rows // 256) * 256
    sem = pltpu.SemaphoreType.DMA
    return pl.pallas_call(
        functools.partial(front_kernel, n_dp, n_pair, pieces, len(shards)),
        out_shape=[
            jax.ShapeDtypeStruct((tokens, width), jnp.bfloat16),
            jax.ShapeDtypeStruct((1, tokens), jnp.int32),
            jax.ShapeDtypeStruct((n_dp, 1, cap), jnp.int32),
        ]
        + [jax.ShapeDtypeStruct((n,) + s.shape, jnp.bfloat16) for s in shards],
        in_specs=[VM, VM, ANY] + [VM] * len(shards),
        out_specs=[VM] * 3 + [ANY] * len(shards),
        scratch_shapes=[
            pltpu.VMEM((n, shards[p[0]].shape[0], p[2] - p[1]), jnp.bfloat16) for p in pieces
        ]
        + [
            pltpu.VMEM((table_rows, width), jnp.float32),
            pltpu.VMEM((padded, width), jnp.bfloat16),
            pltpu.VMEM((n_dp, 8, cap), jnp.float32),
            pltpu.VMEM((n_dp, 8, cap), jnp.float32),
            pltpu.VMEM((n_dp, cap, width), jnp.bfloat16),
            pltpu.VMEM((n_dp, cap, width), jnp.bfloat16),
            pltpu.VMEM((tokens, width), jnp.float32),
            sem,
            sem((2, n_dp)),
            sem((2, n_dp)),
            sem((2, k, hops)),
            sem((2, k, hops + 1)),
            sem((2, k, 2 * hops + 2)),
            sem((k,)),
        ],
        compiler_params=pltpu.CompilerParams(
            collective_id=cid, has_side_effects=True, vmem_limit_bytes=VMEM_LIMIT
        ),
        name="rows_and_weights",
    )(owner, row, table, *shards)


class Scatter:
    def __init__(self, n_dp, n_pair, pieces, ins, outs, boxes, sems):
        self.n_pair, self.pieces, self.ins, self.outs = n_pair, pieces, ins, outs
        k = len(pieces)
        self.acc, self.from_core = boxes[:k], boxes[k : 2 * k]
        self.from_side, self.from_hop = boxes[2 * k : 3 * k], boxes[3 * k :]
        self.load_sem, self.core_sem, self.side_sem, self.hop_sem = sems
        self.me = my_index(n_pair)
        self.hops = (n_dp * n_pair - 1).bit_length() - 2
        self.orders = [bit_order(n_dp, n_pair, piece[3]) for piece in pieces]
        self.count = k

    def source(self, a, block):
        which, low, high, _ = self.pieces[a]
        return self.ins[which].at[block, :, pl.ds(low, high - low)]

    def near(self, bit):
        return place(self.me ^ (1 << bit), self.n_pair)

    def load(self):
        for a in range(self.count):
            for p in range(2 << self.hops):
                pltpu.make_async_copy(
                    self.source(a, self.me ^ offset(self.orders[a], p)),
                    self.acc[a].at[p],
                    self.load_sem.at[a],
                ).start()

    def loaded(self):
        for a in range(self.count):
            pltpu.make_async_copy(self.acc[a], self.acc[a], self.load_sem.at[a]).wait()

    def core(self, a, r, sided, part=None):
        lo, count = stage(r)
        lo = lo + (sided << self.hops)
        to = self.from_core[a].at[pl.ds(lo, count)]
        source = to
        if part is not None:
            to = self.from_core[a].at[lo + part]
            source = self.source(a, self.me ^ (offset(self.orders[a], lo + part) + 1))
        slot = 2 * r + sided
        return remote(
            source, to, self.core_sem.at[0, a, slot], self.core_sem.at[1, a, slot], self.near(0)
        )

    def core_out(self, r):
        for sided in (1, 0):
            for a in range(self.count):
                for part in range(stage(r)[1]):
                    self.core(a, r, sided, part).start()

    def add(self, a, lo, count, box, at):
        acc = self.acc[a]

        def body(j, carry):
            acc[lo + j] = (
                acc[lo + j].astype(jnp.float32) + box[at + j].astype(jnp.float32)
            ).astype(jnp.bfloat16)
            return carry

        lax.fori_loop(0, count, body, 0)

    def side(self, a, r):
        lo, count = stage(r)
        return remote(
            self.acc[a].at[pl.ds((1 << self.hops) + lo, count)],
            self.from_side[a].at[pl.ds(lo, count)],
            self.side_sem.at[0, a, r],
            self.side_sem.at[1, a, r],
            self.near(self.orders[a][self.hops]),
        )

    def hop(self, a, r):
        return remote(
            self.acc[a].at[pl.ds(1 << r, 1 << r)],
            self.from_hop[a].at[pl.ds(self.hop_base(r), 1 << r)],
            self.hop_sem.at[0, a, r],
            self.hop_sem.at[1, a, r],
            self.near(self.orders[a][r]),
        )

    def hop_base(self, r):
        return (1 << self.hops) - (2 << r)

    def core_in(self, r):
        lo, count = stage(r)
        for sided in (1, 0):
            for a in range(self.count):
                self.core(a, r, sided).wait_recv()
                at = lo + (sided << self.hops)
                self.add(a, at, count, self.from_core[a], at)
                if sided:
                    self.side(a, r).start()

    def side_in(self, r):
        lo, count = stage(r)
        for a in range(self.count):
            self.side(a, r).wait_recv()
            self.add(a, lo, count, self.from_side[a], lo)
            if r == self.hops:
                self.hop(a, r - 1).start()

    def hop_in(self, r):
        for a in range(self.count):
            self.hop(a, r).wait_recv()
            base = self.hop_base(r)
            if r:
                mid = 1 << (r - 1)
                self.add(a, mid, mid, self.from_hop[a], base + mid)
                self.hop(a, r - 1).start()
                self.add(a, 0, mid, self.from_hop[a], base)
            else:
                which, low, high, _ = self.pieces[a]
                self.outs[which][:, low:high] = self.acc[a][0].astype(jnp.float32) + self.from_hop[
                    a
                ][base].astype(jnp.float32)

    def finish(self):
        for a in range(self.count):
            for r in range(self.hops):
                self.hop(a, r).wait_send()
            for r in range(self.hops + 1):
                self.side(a, r).wait_send()
                self.core(a, r, 0).wait_send()
                self.core(a, r, 1).wait_send()


def backward_kernel(n_dp, n_pair, pieces, n_in, *refs):
    k_count = len(pieces)
    len_ref, q_ref, k_ref, v_ref, g_ref, w_ref = refs[:6]
    ins = refs[6 : 6 + n_in]
    o_ref, z_ref, square_ref = refs[6 + n_in : 9 + n_in]
    outs = refs[9 + n_in : 9 + 2 * n_in]
    table, total, box, sem = refs[9 + 2 * n_in : 13 + 2 * n_in]
    rest = refs[13 + 2 * n_in :]
    weights = Scatter(n_dp, n_pair, pieces, ins, outs, rest[: 4 * k_count], rest[4 * k_count :])
    at = pl.program_id(0) * pl.num_programs(1) + pl.program_id(1)
    hops = weights.hops

    @pl.when(at == 0)
    def _():
        weights.load()
        greet([weights.near(bit) for bit in range(hops + 2)])
        for r in reversed(range(hops + 1)):
            weights.core_out(r)

    @pl.when(at == 2)
    def _():
        weights.loaded()
        weights.core_in(hops)

    @pl.when(at == 3)
    def _():
        for r in reversed(range(hops)):
            weights.core_in(r)

    @pl.when(at == 6)
    def _():
        weights.side_in(hops)

    @pl.when(at == 7)
    def _():
        for r in reversed(range(hops)):
            weights.side_in(r)

    seq = q_ref.shape[0]
    tiles = seq // 128
    doc = pl.program_id(1)
    @pl.when(doc == 0)
    def _():
        for h in range(2):
            band(w_ref, 2 * pl.program_id(0) + h, h, table, seq)
        total[...] = jnp.zeros_like(total)
    length = len_ref[doc]
    lane = lax.broadcasted_iota(jnp.int32, (seq, 128), 1)
    row = lax.broadcasted_iota(jnp.int32, (seq, 1), 0)
    q = q_ref[...] * jnp.bfloat16(0.125)
    k = k_ref[...]
    v = v_ref[...]
    g = g_ref[...]
    parts = []
    for h in range(2):
        mine = (lane < 64) == (h == 0)
        s = lax.dot_general(k, jnp.where(mine, q, 0), NT, preferred_element_type=jnp.float32)
        s = jnp.where(row < length, s + table[h], -1000000000.0)
        e = jnp.exp(s - jnp.max(s, axis=0, keepdims=True))
        p = e * (1.0 / jnp.sum(e, axis=0, keepdims=True))
        dv = jnp.dot(p.astype(jnp.bfloat16), g, preferred_element_type=jnp.float32)
        dp = lax.dot_general(v, jnp.where(mine, g, 0), NT, preferred_element_type=jnp.float32)
        ds = (p * (dp - jnp.sum(p * dp, axis=0, keepdims=True))).astype(jnp.bfloat16)
        total[h] += ds.astype(jnp.float32)
        dk = jnp.dot(ds, q, preferred_element_type=jnp.float32)
        dq = lax.dot_general(ds, k, TN, preferred_element_type=jnp.float32) * 0.125
        parts.append((dq, dk, dv))
    pair, pairs, docs = pl.program_id(0), pl.num_programs(0), pl.num_programs(1)
    step = pair * docs + doc
    slot = lax.rem(step, 2)

    def out(i):
        rows = pl.ds(pl.multiple_of(doc * seq, seq), seq)
        columns = pl.ds(pl.multiple_of((i * pairs + pair) * 128, 128), 128)
        return pltpu.make_async_copy(box.at[slot, i], o_ref.at[rows, columns], sem.at[slot, i])

    for i in range(3):
        @pl.when(step >= 2)
        def _():
            out(i).wait()
        box[slot, i] = jnp.where(lane < 64, parts[0][i], parts[1][i]).astype(o_ref.dtype)
        out(i).start()

    for r in range(1, hops):
        @pl.when(step == pairs * docs - 1 - r)
        def _():
            weights.hop_in(r)

    @pl.when(step == pairs * docs - 1)
    def _():
        weights.hop_in(0)
        weights.finish()
        square_ref[...] = jnp.zeros_like(square_ref)
        for ref in outs:
            square = jnp.sum(ref[...] * ref[...], axis=0, keepdims=True)
            square_ref[...] += jnp.sum(square, axis=1, keepdims=True)
        for i in range(3):
            out(i).wait()
            pltpu.make_async_copy(box.at[1 - slot, i], box.at[1 - slot, i], sem.at[1 - slot, i]).wait()
    @pl.when(doc == pl.num_programs(1) - 1)
    def _():
        r = lax.broadcasted_iota(jnp.int32, (128, 128), 0)
        c = lax.broadcasted_iota(jnp.int32, (128, 128), 1)
        flip = jnp.where(r + c == 127, 1.0, 0.0)
        z_ref[...] = jnp.zeros_like(z_ref)
        for h in range(2):
            def block(d):
                return sum(total[h, a * 128 : a * 128 + 128, (a - d) * 128 : (a - d) * 128 + 128] for a in range(tiles) if 0 <= a - d < tiles)
            for d in (-1, 0, 1):
                x = jnp.dot(flip, block(d), precision=HIGHEST, preferred_element_type=jnp.float32)
                x = jnp.concatenate([x, jnp.zeros_like(x)], axis=1)
                x = pltpu.roll(x, 0, 1, stride=1, stride_axis=0)
                z_ref[0, h, d + 1 : d + 2, :] = jnp.sum(x, axis=0, keepdims=True)
            z_ref[0, h, 3:4, 0:128] = jnp.sum(sum(block(-d) for d in range(2, tiles)), axis=0, keepdims=True)
            z_ref[0, h, 4:5, 0:128] = jnp.sum(sum(block(d) for d in range(2, tiles)), axis=0, keepdims=True)

def attention_back(lengths, qkv, g, w, seq, grads, pieces, cid):
    n_dp, n_pair = lax.axis_size("dp"), lax.axis_size("pair")
    tokens = qkv.shape[0]
    pairs = w.shape[0] // 2
    docs = tokens // seq
    spec = lambda base: pl.BlockSpec((seq, 128), lambda h, d, *_: (d, base + h))
    still = lambda shape: pl.BlockSpec(shape, lambda h, d, *_: (0, 0))
    boxes, sems = scatter_scratch(n_dp * n_pair, grads, pieces)
    return pl.pallas_call(
        functools.partial(backward_kernel, n_dp, n_pair, pieces, len(grads)),
        grid_spec=pltpu.PrefetchScalarGridSpec(
            num_scalar_prefetch=1,
            grid=(pairs, docs),
            in_specs=[spec(0), spec(pairs), spec(2 * pairs), spec(0), still(w.shape)]
            + [ANY] * len(grads),
            out_specs=[
                ANY,
                pl.BlockSpec((1, 2, 8, 256), lambda h, d, *_: (h, 0, 0, 0)),
                still((1, 1)),
            ]
            + [still(grad.shape[1:]) for grad in grads],
            scratch_shapes=[
                pltpu.VMEM((2, seq, seq), jnp.float32),
                pltpu.VMEM((2, seq, seq), jnp.float32),
                pltpu.VMEM((2, 3, seq, 128), jnp.bfloat16),
                pltpu.SemaphoreType.DMA((2, 3)),
            ]
            + boxes
            + sems,
        ),
        out_shape=[
            jax.ShapeDtypeStruct((tokens, 3 * pairs * 128), jnp.bfloat16),
            jax.ShapeDtypeStruct((pairs, 2, 8, 256), jnp.float32),
            jax.ShapeDtypeStruct((1, 1), jnp.float32),
        ]
        + [jax.ShapeDtypeStruct(grad.shape[1:], jnp.float32) for grad in grads],
        compiler_params=pltpu.CompilerParams(
            dimension_semantics=("arbitrary", "arbitrary"),
            collective_id=cid,
            has_side_effects=True,
            vmem_limit_bytes=VMEM_LIMIT,
        ),
        name="attention_back",
    )(lengths, qkv, qkv, qkv, g, w, *grads)


def back_kernel(n_dp, n_pair, pieces, n_in, chunk, *refs):
    k = len(pieces)
    grad_ref, key_ref, ask_ref, squares_ref = refs[:4]
    ins = refs[4 : 4 + n_in]
    out_ref, square_ref = refs[4 + n_in : 6 + n_in]
    outs = refs[6 + n_in : 6 + 2 * n_in]
    rest = refs[6 + 2 * n_in :]
    boxes, rest = rest[: 4 * k], rest[4 * k :]
    rows_out, rows_in, hot, part, stage_out, got_core, out_side, got_side, other = rest[:9]
    row_sem, core_sem, side_sem, last_sem, out_sem, *sems = rest[9:]
    dp, pair = lax.axis_index("dp"), lax.axis_index("pair")
    core = lax.rem(pair, 2)
    weights = Scatter(n_dp, n_pair, pieces, ins, outs, boxes, sems)
    groups, _, cap, width = rows_out.shape
    slots = ask_ref.shape[1]
    count = stage_out.shape[1]
    half = count * chunk
    tokens = key_ref.shape[1]
    peers = [{"dp": dp ^ j, "pair": pair} for j in range(1, n_dp)]
    partner, across = {"dp": dp, "pair": pair ^ 1}, {"dp": dp, "pair": pair ^ 2}
    weights.load()
    sem = pltpu.get_barrier_semaphore()
    for target in peers + [partner, across]:
        pl.semaphore_signal(sem, inc=1, device_id=target, device_id_type=MESH)

    def row(g, j):
        return remote(
            rows_out.at[g, j],
            rows_in.at[g, pl.ds(pl.multiple_of(j * cap, cap), cap)],
            row_sem.at[0, g, j],
            row_sem.at[1, g, j],
            {"dp": dp ^ j, "pair": pair},
        )

    def loop(size, body):
        def turn(i, carry):
            body(i)
            return carry

        lax.fori_loop(0, size, turn, 0)

    far = sorted(range(1, n_dp), reverse=True)

    pl.semaphore_wait(sem, n_dp + 1)

    def rows_of(t):
        j = n_dp - 1 - t
        slot = lax.broadcasted_iota(jnp.int32, (cap, tokens), 0) + (dp ^ j) * cap
        hits = jnp.where(slot == key_ref[...], 1.0, 0.0).astype(jnp.bfloat16)
        got = jnp.dot(hits, grad_ref[...], preferred_element_type=jnp.float32)
        got = got.astype(jnp.bfloat16)
        for g in range(groups):
            rows_out[g, j] = got[:, g * width : (g + 1) * width]

        @pl.when(j > 0)
        def _():
            row(0, j).start()

    loop(n_dp, rows_of)
    for g in range(1, groups):
        for j in far:
            row(g, j).start()
    for g in range(groups):
        rows_in[g, 0:cap] = rows_out[g, 0]
    for r in reversed(range(weights.hops + 1)):
        weights.core_out(r)

    def tell(c):
        ids = lax.broadcasted_iota(jnp.int32, (chunk, slots), 0) + c * chunk
        hot[c] = jnp.where(ids == ask_ref[...], 1.0, 0.0).astype(jnp.bfloat16)

    loop(2 * count, tell)

    def summed(g, c):
        return jnp.dot(hot[c], rows_in[g], preferred_element_type=jnp.float32)

    def to_core(g, i):
        return remote(
            stage_out.at[g, i], got_core.at[g, i], core_sem.at[0, g, i], core_sem.at[1, g, i], partner
        )

    def to_side(g, i):
        return remote(
            out_side.at[g, i], got_side.at[g, i], side_sem.at[0, g, i], side_sem.at[1, g, i], across
        )

    def to_other(g, i):
        return remote(
            out_side.at[g, i], other.at[g, i], last_sem.at[0, g, i], last_sem.at[1, g, i], partner
        )

    def write_out(box, g, i, which):
        rows = pl.ds(pl.multiple_of(which * half + i * chunk, chunk), chunk)
        return pltpu.make_async_copy(
            box.at[g, i], out_ref.at[rows, pl.ds(g * width, width)], out_sem.at[g, i]
        )

    def local_sums(g):
        for j in far:
            row(g, j).wait_recv()

        def combine(i):
            to_core(g, i).wait_recv()
            out_side[g, i] = (part[i] + got_core[g, i].astype(jnp.float32)).astype(jnp.bfloat16)
            to_side(g, i).start()

        def one(i):
            stage_out[g, i] = summed(g, (1 - core) * count + i).astype(jnp.bfloat16)
            to_core(g, i).start()
            part[i] = summed(g, core * count + i)

            @pl.when(i > 0)
            def _():
                combine(i - 1)

        loop(count, one)
        combine(count - 1)

    square_ref[...] = squares_ref[...]

    def finish_sums(g):
        def one(i):
            to_side(g, i).wait()
            wide = out_side[g, i].astype(jnp.float32) + got_side[g, i].astype(jnp.float32)
            value = wide.astype(jnp.bfloat16)
            out_side[g, i] = value
            to_other(g, i).start()
            write_out(out_side, g, i, core).start()
            wide = value.astype(jnp.float32)
            square = jnp.sum(wide * wide, axis=0, keepdims=True)
            square = jnp.sum(square, axis=1, keepdims=True)
            square_ref[...] += jnp.where(pair < 2, square, 0.0)

        loop(count, one)

    def hand_over(g):
        def one(i):
            to_other(g, i).wait_recv()
            write_out(out_side, g, i, core).wait()
            write_out(other, g, i, 1 - core).start()

        loop(count, one)

    weights.loaded()
    for r in reversed(range(weights.hops + 1)):
        weights.core_in(r)
    for g in range(groups):
        local_sums(g)
        if g:
            finish_sums(g - 1)
        if g == groups // 2:
            for r in reversed(range(weights.hops + 1)):
                weights.side_in(r)
    for r in reversed(range(1, weights.hops)):
        weights.hop_in(r)
    finish_sums(groups - 1)
    weights.hop_in(0)
    for ref in outs:
        square = jnp.sum(ref[...] * ref[...], axis=0, keepdims=True)
        square_ref[...] += jnp.sum(square, axis=1, keepdims=True)
    for g in range(groups):
        hand_over(g)
    for g in range(groups):
        for j in far:
            row(g, j).wait_send()

        def one(i):
            to_core(g, i).wait_send()
            to_other(g, i).wait_send()
            write_out(other, g, i, 1 - core).wait()

        loop(count, one)
    weights.finish()


def scatter_scratch(n, grads, pieces):
    k, hops, sem = len(pieces), (n - 1).bit_length() - 2, pltpu.SemaphoreType.DMA
    boxes = [
        pltpu.VMEM((lead, grads[p[0]].shape[1], p[2] - p[1]), jnp.bfloat16)
        for lead in (n // 2, n // 2, n // 4, n // 4 - 1)
        for p in pieces
    ]
    return boxes, [
        sem((k,)),
        sem((2, k, 2 * hops + 2)),
        sem((2, k, hops + 1)),
        sem((2, k, hops)),
    ]


def back(grad, key, asked, squares, grads, pieces, table_rows, groups, cid):
    n_dp, n_pair = lax.axis_size("dp"), lax.axis_size("pair")
    boxes, sems = scatter_scratch(n_dp * n_pair, grads, pieces)
    chunk = 512
    rows = -(-table_rows // (2 * chunk)) * 2 * chunk
    count = rows // 2 // chunk
    tokens, full = grad.shape
    width = full // groups
    slots = asked.shape[1]
    cap = slots // n_dp
    sem = pltpu.SemaphoreType.DMA
    box = pltpu.VMEM((groups, count, chunk, width), jnp.bfloat16)

    return pl.pallas_call(
        functools.partial(back_kernel, n_dp, n_pair, pieces, len(grads), chunk),
        out_shape=[
            jax.ShapeDtypeStruct((rows, full), jnp.bfloat16),
            jax.ShapeDtypeStruct((1, 1), jnp.float32),
        ]
        + [jax.ShapeDtypeStruct(g.shape[1:], jnp.float32) for g in grads],
        in_specs=[VM] * 4 + [ANY] * len(grads),
        out_specs=[ANY, VM] + [VM] * len(grads),
        scratch_shapes=boxes
        + [
            pltpu.VMEM((groups, n_dp, cap, width), jnp.bfloat16),
            pltpu.VMEM((groups, slots, width), jnp.bfloat16),
            pltpu.VMEM((2 * count, chunk, slots), jnp.bfloat16),
            pltpu.VMEM((count, chunk, width), jnp.float32),
            box,
            box,
            box,
            box,
            box,
            sem((2, groups, n_dp)),
            sem((2, groups, count)),
            sem((2, groups, count)),
            sem((2, groups, count)),
            sem((groups, count)),
        ]
        + sems,
        compiler_params=pltpu.CompilerParams(
            collective_id=cid, has_side_effects=True, vmem_limit_bytes=VMEM_LIMIT
        ),
        name="table_and_weights",
    )(grad, key, asked, squares, *grads)


BIAS_CORRECT = (1.0 - beta_one**STEP, 1.0 - beta_two**STEP)


def adam_parts(weight, first, second, grad, factor, rate, shrink):
    clipped = grad * factor
    first_new = beta_one * first + (1.0 - beta_one) * clipped
    second_new = beta_two * second + (1.0 - beta_two) * (clipped * clipped)
    root = jnp.sqrt(second_new * (1.0 / BIAS_CORRECT[1])) + adam_eps
    step = (rate / BIAS_CORRECT[0]) * first_new / root
    return (weight * (1.0 - rate * shrink) - step, first_new, second_new)


def packed_base(gains, width):
    return -(-gains * width // 128 // 8) * 8


def norm_kernel(n_dp, n_pair, n_gain, *refs):
    gain_refs = refs[:n_gain]
    bias_ref, square_ref, total_ref, block, by_dp, by_pair = refs[n_gain : n_gain + 6]
    rounds = Rounds(n_dp, n_pair, *refs[n_gain + 6 :])
    width = gain_refs[0].shape[1]
    base = packed_base(n_gain, width)
    block[...] = jnp.zeros_like(block)
    for c in range(width // 128):
        for g in range(n_gain):
            at = c * n_gain + g
            block[at : at + 1, :] = gain_refs[g][:, c * 128 : (c + 1) * 128]
    block[base : base + bias_ref.shape[0], : bias_ref.shape[1]] = bias_ref[...]
    block[base : base + 1, 127:128] = square_ref[...]
    rounds.entered()
    rounds.over_dp(block, by_dp)
    total = by_dp[0]
    for d in range(1, n_dp):
        total = total + by_dp[d]
    block[...] = total
    rounds.over_pair(block, by_pair)
    total = by_pair[0]
    for p in range(1, n_pair):
        total = total + by_pair[p]
    total_ref[...] = total


def small_total(gain_grads, bias_grad, square, cid):
    n_dp, n_pair = lax.axis_size("dp"), lax.axis_size("pair")
    count, width = len(gain_grads), gain_grads[0].shape[1]
    height = -(-(packed_base(count, width) + bias_grad.shape[0]) // 8) * 8
    return pl.pallas_call(
        functools.partial(norm_kernel, n_dp, n_pair, count),
        out_shape=jax.ShapeDtypeStruct((height, 128), jnp.float32),
        in_specs=[VM] * (count + 2),
        out_specs=VM,
        scratch_shapes=[
            pltpu.VMEM((height, 128), jnp.float32),
            pltpu.VMEM((n_dp, height, 128), jnp.float32),
            pltpu.VMEM((n_pair, height, 128), jnp.float32),
        ]
        + round_sems(n_dp, n_pair),
        compiler_params=pltpu.CompilerParams(collective_id=cid, has_side_effects=True),
        name="small_total",
    )(*gain_grads, bias_grad, square)


def update_kernel(mats, *refs):
    total_ref, loss_ref, low = refs[:3]
    table, small = refs[3:6], refs[6:12]
    grads = refs[12 : 12 + mats]
    states = refs[12 + mats : 12 + 4 * mats]
    rest = refs[12 + 4 * mats :]
    norm_out, loss_out, table_out, small_out = rest[0], rest[1], rest[2:5], rest[5:11]
    mat_out = rest[11:]
    gains, width = small[0].shape
    base = packed_base(gains, width)
    total = total_ref[...]
    row = lax.broadcasted_iota(jnp.int32, total.shape, 0)
    lane = lax.broadcasted_iota(jnp.int32, total.shape, 1)
    plain = jnp.where((row == base) & (lane == 127), total, total * total)
    norm = jnp.sqrt(jnp.sum(jnp.sum(plain, axis=1, keepdims=True), axis=0, keepdims=True))
    factor = jnp.minimum(1.0, clip_limit / norm)
    step = pl.program_id(0)

    @pl.when(step == 0)
    def _():
        norm_out[...] = norm
        loss_out[...] = loss_ref[...]
        for c in range(width // 128):
            columns = slice(c * 128, (c + 1) * 128)
            grad = total_ref[c * gains : (c + 1) * gains, :]
            new = adam_parts(*(ref[:, columns] for ref in small[:3]), grad, factor, 1.0, 0.0)
            for ref, value in zip(small_out[:3], new):
                ref[:, columns] = value
        heads = small[3].shape[1]
        grad = total_ref[base : base + small[3].shape[0], :heads]
        new = adam_parts(*(ref[...] for ref in small[3:]), grad, factor, 0.3, 0.0)
        for ref, value in zip(small_out[3:], new):
            ref[...] = value

    for which in range(mats):
        three = slice(3 * which, 3 * which + 3)
        new = adam_parts(*(ref[...] for ref in states[three]), grads[which][...], factor, 0.05, 0.01)
        for ref, value in zip(mat_out[three], new):
            ref[...] = value

    def body(j, carry):
        rows = pl.ds(pl.multiple_of(j * 16, 16), 16)
        new = adam_parts(*(ref[rows] for ref in table), low[rows].astype(jnp.float32), factor, 1.0, 0.01)
        for ref, value in zip(table_out, new):
            ref[rows] = value
        return carry

    lax.fori_loop(0, low.shape[0] // 16, body, 0)


def update(total, loss, table_grad, table, small, grads, states):
    rows, width = table[0].shape
    steps = 6
    tall = -(-rows // steps // 16) * 16
    flat = [array for group in states for array in group]
    like = lambda array: jax.ShapeDtypeStruct(array.shape, jnp.float32)
    whole = lambda array: pl.BlockSpec(array.shape, lambda i: (0, 0))
    table_spec = pl.BlockSpec((tall, width), lambda i: (i, 0))

    def part(array):
        if array.shape[1] % (128 * steps) == 0 and array.shape[0] < 32:
            return pl.BlockSpec((array.shape[0], array.shape[1] // steps), lambda i: (0, i))
        if array.shape[0] % (8 * steps) == 0:
            return pl.BlockSpec((array.shape[0] // steps, array.shape[1]), lambda i: (i, 0))
        return whole(array)

    return pl.pallas_call(
        functools.partial(update_kernel, len(grads)),
        grid=(steps,),
        out_shape=[like(loss), like(loss)] + [like(array) for array in (*table, *small, *flat)],
        in_specs=[whole(total), whole(loss)]
        + [table_spec] * 4
        + [whole(array) for array in small]
        + [part(array) for array in (*grads, *flat)],
        out_specs=[whole(loss)] * 2
        + [table_spec] * 3
        + [whole(array) for array in small]
        + [part(array) for array in flat],
        compiler_params=pltpu.CompilerParams(
            dimension_semantics=("arbitrary",), vmem_limit_bytes=VMEM_LIMIT
        ),
        name="update",
    )(total, loss, table_grad, *table, *small, *grads, *flat)


def local_plain(
    token_owner,
    token_row,
    lengths,
    positives,
    negatives,
    neg_counts,
    embed_table,
    embed_first,
    embed_second,
    qkv_weight,
    qkv_first,
    qkv_second,
    out_weight,
    out_first,
    out_second,
    in_weight,
    in_first,
    in_second,
    down_weight,
    down_first,
    down_second,
    norm_gains,
    gains_first,
    gains_second,
    position_bias,
    bias_first,
    bias_second,
):
    doc_count = lengths.shape[0]
    seq_len = token_row.shape[1]
    model_width = embed_table.shape[1]
    head_count = position_bias.shape[1]
    bucket_count = position_bias.shape[0]
    tok_total = doc_count * seq_len
    owners = lax.axis_size("dp")
    capacity = max(2, 2 * tok_total // owners)
    low_mats = (
        qkv_weight.astype(jnp.bfloat16),
        out_weight.astype(jnp.bfloat16),
        in_weight.astype(jnp.bfloat16),
        down_weight.astype(jnp.bfloat16),
    )
    qkv_full, out_full, in_full, down_full = (
        lax.all_gather(low_mats[0], ("dp", "pair"), axis=0, tiled=True),
        lax.all_gather(low_mats[1], ("dp", "pair"), axis=0, tiled=True),
        lax.all_gather(low_mats[2], ("dp", "pair"), axis=0, tiled=True),
        lax.all_gather(low_mats[3], ("dp", "pair"), axis=0, tiled=True),
    )
    tok_owner = token_owner.reshape(-1)
    tok_row = token_row.reshape(-1)
    owner_hits = (tok_owner[:, None] == jnp.arange(owners, dtype=jnp.int32)[None, :]).astype(
        jnp.int32
    )
    slot_rank = jnp.sum((jnp.cumsum(owner_hits, axis=0) - 1) * owner_hits, axis=1)
    requests = jnp.zeros((owners, capacity), jnp.int32).at[tok_owner, slot_rank].set(tok_row)
    asked_rows = lax.all_to_all(requests, "dp", split_axis=0, concat_axis=0, tiled=True)
    looked = jnp.take(embed_table, asked_rows.reshape(-1), axis=0).astype(jnp.bfloat16)
    answer = lax.all_to_all(
        looked.reshape(asked_rows.shape + (model_width,)),
        "dp",
        split_axis=0,
        concat_axis=0,
        tiled=True,
    )
    replies, asked_rows = (answer, asked_rows)
    embedded = replies[tok_owner, slot_rank].astype(jnp.float32)
    positions = jnp.arange(seq_len)
    live = positions[None, :] < lengths[:, None]
    pair_buckets = bucket_of(
        (positions[None, :] - positions[:, None]).reshape(-1), bucket_count, REACH
    )
    pair_hits = (jnp.arange(bucket_count)[:, None] == pair_buckets[None, :]).astype(jnp.float32)
    bias_full = jnp.dot(position_bias.T, pair_hits, precision=HIGHEST).reshape(
        head_count, seq_len, seq_len
    )
    bucket_map = pair_hits.astype(jnp.bfloat16)

    def split_doc(source, doc_index):
        doc_rows = source[doc_index * seq_len : (doc_index + 1) * seq_len]
        return tuple(
            (
                doc_rows[:, member * model_width : (member + 1) * model_width].reshape(
                    seq_len, head_count, -1
                )
                for member in range(3)
            )
        )

    normed_one, inverse_one = rms_forward(embedded, norm_gains[0])
    normed_one = normed_one.astype(jnp.bfloat16)
    qkv_rows = jnp.dot(normed_one, qkv_full, preferred_element_type=jnp.float32).astype(
        jnp.bfloat16
    )
    attended_parts = []
    logsum_parts = []
    for doc_index in range(doc_count):
        query_heads, key_heads, value_heads = split_doc(qkv_rows, doc_index)
        doc_out, logsum = attend_forward(
            query_heads, key_heads, value_heads, bias_full, live[doc_index]
        )
        attended_parts.append(doc_out.reshape(seq_len, model_width))
        logsum_parts.append(logsum)
    attended = jnp.concatenate(attended_parts, axis=0).astype(jnp.bfloat16)
    residual = embedded + jnp.dot(attended, out_full, preferred_element_type=jnp.float32)
    normed_two, inverse_two = rms_forward(residual, norm_gains[1])
    normed_two = normed_two.astype(jnp.bfloat16)
    hidden = jax.nn.relu(jnp.dot(normed_two, in_full, preferred_element_type=jnp.float32)).astype(
        jnp.bfloat16
    )
    output_rows = residual + jnp.dot(hidden, down_full, preferred_element_type=jnp.float32)
    normed_three, inverse_three = rms_forward(output_rows, norm_gains[2])
    live_rows = live.reshape(-1, 1)
    length_float = lengths.astype(jnp.float32)
    pooled_local = (
        jnp.sum(
            jnp.where(live_rows, normed_three, 0.0).reshape(doc_count, seq_len, model_width), axis=1
        )
        / length_float[:, None]
    )
    pooled_all = lax.all_gather(pooled_local, ("dp", "pair"), axis=0, tiled=True)
    loss_value, loss_pullback = jax.vjp(
        lambda pooled_in: margin_loss(pooled_in, positives, negatives, neg_counts), pooled_all
    )
    grad_pooled_all = loss_pullback(jnp.ones((), jnp.float32))[0]
    grad_pooled = lax.dynamic_slice_in_dim(
        grad_pooled_all, lax.axis_index(("dp", "pair")) * doc_count, doc_count, 0
    )
    grad_three = jnp.where(
        live_rows, jnp.repeat(grad_pooled / length_float[:, None], seq_len, axis=0), 0.0
    )
    qkv_back, out_back, in_back, down_back = (qkv_full, out_full, in_full, down_full)
    grad_output, gain_three = rms_backward(output_rows, inverse_three, norm_gains[2], grad_three)
    grad_branch = grad_output.astype(jnp.bfloat16)
    grad_down = lax.dot_general(
        hidden, grad_branch, CONTRACT_ROWS, preferred_element_type=jnp.float32
    )
    grad_hidden = lax.dot_general(
        grad_branch, down_back, CONTRACT_COLS, preferred_element_type=jnp.float32
    )
    grad_pre = jnp.where(hidden > 0, grad_hidden, 0.0).astype(jnp.bfloat16)
    grad_in = lax.dot_general(
        normed_two, grad_pre, CONTRACT_ROWS, preferred_element_type=jnp.float32
    )
    grad_normed_two = lax.dot_general(
        grad_pre, in_back, CONTRACT_COLS, preferred_element_type=jnp.float32
    )
    grad_res_part, gain_two = rms_backward(residual, inverse_two, norm_gains[1], grad_normed_two)
    grad_residual = grad_output + grad_res_part
    grad_attn_branch = grad_residual.astype(jnp.bfloat16)
    grad_out = lax.dot_general(
        attended, grad_attn_branch, CONTRACT_ROWS, preferred_element_type=jnp.float32
    )
    grad_attended = lax.dot_general(
        grad_attn_branch, out_back, CONTRACT_COLS, preferred_element_type=jnp.float32
    ).astype(jnp.bfloat16)
    grad_qkv_parts = []
    bias_grad_heads = jnp.zeros((head_count, bucket_count), jnp.float32)
    for doc_index in range(doc_count):
        query_heads, key_heads, value_heads = split_doc(qkv_rows, doc_index)
        grad_doc = grad_attended[doc_index * seq_len : (doc_index + 1) * seq_len].reshape(
            seq_len, head_count, -1
        )
        grad_query, grad_key, grad_value, grad_low = attend_backward(
            query_heads,
            key_heads,
            value_heads,
            bias_full,
            live[doc_index],
            logsum_parts[doc_index],
            grad_doc,
        )
        grad_qkv_parts.append(
            jnp.concatenate(
                [
                    grad_query.reshape(seq_len, model_width),
                    grad_key.reshape(seq_len, model_width),
                    grad_value.reshape(seq_len, model_width),
                ],
                axis=1,
            )
        )
        bias_grad_heads = bias_grad_heads + lax.dot_general(
            grad_low.reshape(head_count, -1),
            bucket_map,
            CONTRACT_COLS,
            preferred_element_type=jnp.float32,
        )
    bias_grad_local = bias_grad_heads.T
    grad_qkv_rows = jnp.concatenate(grad_qkv_parts, axis=0).astype(jnp.bfloat16)
    grad_qkv = lax.dot_general(
        normed_one, grad_qkv_rows, CONTRACT_ROWS, preferred_element_type=jnp.float32
    )
    grad_normed_one = lax.dot_general(
        grad_qkv_rows, qkv_back, CONTRACT_COLS, preferred_element_type=jnp.float32
    )
    grad_emb_part, gain_one = rms_backward(embedded, inverse_one, norm_gains[0], grad_normed_one)
    grad_embedded = grad_residual + grad_emb_part
    sendback = (
        jnp.zeros((owners, capacity, model_width), jnp.float32)
        .at[tok_owner, slot_rank]
        .set(grad_embedded)
    )
    arrived = lax.all_to_all(sendback, "dp", split_axis=0, concat_axis=0, tiled=True)
    table_grad = jax.ops.segment_sum(
        arrived.reshape(-1, model_width), asked_rows.reshape(-1), num_segments=embed_table.shape[0]
    )
    table_grad = lax.psum(table_grad, "pair")
    weight_grads = (
        lax.psum_scatter(grad_qkv, ("dp", "pair"), scatter_dimension=0, tiled=True),
        lax.psum_scatter(grad_out, ("dp", "pair"), scatter_dimension=0, tiled=True),
        lax.psum_scatter(grad_in, ("dp", "pair"), scatter_dimension=0, tiled=True),
        lax.psum_scatter(grad_down, ("dp", "pair"), scatter_dimension=0, tiled=True),
    )
    pair_first = (lax.axis_index("pair") == 0).astype(jnp.float32)
    square_part = jnp.sum(
        jnp.stack([jnp.sum(grad_piece * grad_piece) for grad_piece in weight_grads])
    ) + pair_first * jnp.sum(table_grad * table_grad)
    gain_grad, bias_grad, square_sum = lax.psum(
        (jnp.stack([gain_one, gain_two, gain_three]), bias_grad_local, square_part), ("dp", "pair")
    )
    clip_norm = jnp.sqrt(
        square_sum + jnp.sum(gain_grad * gain_grad) + jnp.sum(bias_grad * bias_grad)
    )
    factor = jnp.minimum(1.0, clip_limit / clip_norm)
    table_out = adam_step(embed_table, embed_first, embed_second, table_grad * factor, 1.0, 0.01)
    qkv_out = adam_step(qkv_weight, qkv_first, qkv_second, weight_grads[0] * factor, 0.05, 0.01)
    out_out = adam_step(out_weight, out_first, out_second, weight_grads[1] * factor, 0.05, 0.01)
    in_out = adam_step(in_weight, in_first, in_second, weight_grads[2] * factor, 0.05, 0.01)
    down_out = adam_step(down_weight, down_first, down_second, weight_grads[3] * factor, 0.05, 0.01)
    gains_out = adam_step(norm_gains, gains_first, gains_second, gain_grad * factor, 1.0, 0.0)
    bias_out = adam_step(position_bias, bias_first, bias_second, bias_grad * factor, 0.3, 0.0)
    return (
        loss_value,
        clip_norm,
        table_out[0],
        table_out[1],
        table_out[2],
        qkv_out[0],
        qkv_out[1],
        qkv_out[2],
        out_out[0],
        out_out[1],
        out_out[2],
        in_out[0],
        in_out[1],
        in_out[2],
        down_out[0],
        down_out[1],
        down_out[2],
        gains_out[0],
        gains_out[1],
        gains_out[2],
        bias_out[0],
        bias_out[1],
        bias_out[2],
    )


def local_fast(
    token_owner,
    token_row,
    lengths,
    positives,
    negatives,
    neg_counts,
    embed_table,
    embed_first,
    embed_second,
    qkv_weight,
    qkv_first,
    qkv_second,
    out_weight,
    out_first,
    out_second,
    in_weight,
    in_first,
    in_second,
    down_weight,
    down_first,
    down_second,
    norm_gains,
    gains_first,
    gains_second,
    position_bias,
    bias_first,
    bias_second,
):
    doc_count = lengths.shape[0]
    seq_len = token_row.shape[1]
    model_width = embed_table.shape[1]
    head_count = position_bias.shape[1]
    bucket_count = position_bias.shape[0]
    tok_total = doc_count * seq_len
    owners = lax.axis_size("dp")
    capacity = max(2, 2 * tok_total // owners)
    holders = lax.axis_size("pair")
    shards = (qkv_weight, out_weight, in_weight, down_weight)
    embedded_low, slot_keys, asked_rows, *full = front(
        token_owner.reshape(1, -1),
        token_row.reshape(1, -1),
        embed_table,
        shards,
        weight_pieces([shard.shape[1] for shard in shards]),
        capacity,
        owners,
        holders,
        1,
    )
    qkv_full, out_full, in_full, down_full = (
        matrix.reshape(-1, matrix.shape[2]) for matrix in full
    )
    embedded = embedded_low.astype(jnp.float32)
    positions = jnp.arange(seq_len)
    live = positions[None, :] < lengths[:, None]
    normed_one, inverse_one = rms_forward(embedded, norm_gains[0])
    normed_one = normed_one.astype(jnp.bfloat16)
    qkv_rows = jnp.dot(normed_one, qkv_full, preferred_element_type=jnp.float32).astype(
        jnp.bfloat16
    )
    attended = attention(lengths, qkv_rows, bias_rows(position_bias.T, seq_len, 1), seq_len)
    residual = embedded + jnp.dot(attended, out_full, preferred_element_type=jnp.float32)
    normed_two, inverse_two = rms_forward(residual, norm_gains[1])
    normed_two = normed_two.astype(jnp.bfloat16)
    hidden = jax.nn.relu(jnp.dot(normed_two, in_full, preferred_element_type=jnp.float32)).astype(
        jnp.bfloat16
    )
    output_rows = residual + jnp.dot(hidden, down_full, preferred_element_type=jnp.float32)
    normed_three, inverse_three = rms_forward(output_rows, norm_gains[2])
    live_rows = live.reshape(-1, 1)
    length_float = lengths.astype(jnp.float32)
    pooled_local = (
        jnp.sum(
            jnp.where(live_rows, normed_three, 0.0).reshape(doc_count, seq_len, model_width), axis=1
        )
        / length_float[:, None]
    )
    loss_cell, grad_pooled = pooled_loss(
        pooled_local, positives, negatives, neg_counts, 3
    )
    grad_three = jnp.where(
        live_rows, jnp.repeat(grad_pooled / length_float[:, None], seq_len, axis=0), 0.0
    )
    qkv_back, out_back, in_back, down_back = (qkv_full, out_full, in_full, down_full)
    grad_output, gain_three = rms_backward(output_rows, inverse_three, norm_gains[2], grad_three)
    grad_branch = grad_output.astype(jnp.bfloat16)
    grad_down = lax.dot_general(
        hidden, grad_branch, CONTRACT_ROWS, preferred_element_type=jnp.float32
    )
    grad_hidden = lax.dot_general(
        grad_branch, down_back, CONTRACT_COLS, preferred_element_type=jnp.float32
    )
    grad_pre = jnp.where(hidden > 0, grad_hidden, 0.0).astype(jnp.bfloat16)
    grad_in = lax.dot_general(
        normed_two, grad_pre, CONTRACT_ROWS, preferred_element_type=jnp.float32
    )
    grad_normed_two = lax.dot_general(
        grad_pre, in_back, CONTRACT_COLS, preferred_element_type=jnp.float32
    )
    grad_res_part, gain_two = rms_backward(residual, inverse_two, norm_gains[1], grad_normed_two)
    grad_residual = grad_output + grad_res_part
    grad_attn_branch = grad_residual.astype(jnp.bfloat16)
    grad_out = lax.dot_general(
        attended, grad_attn_branch, CONTRACT_ROWS, preferred_element_type=jnp.float32
    )
    grad_attended = lax.dot_general(
        grad_attn_branch, out_back, CONTRACT_COLS, preferred_element_type=jnp.float32
    ).astype(jnp.bfloat16)
    parts = owners * holders

    def blocks(*grads):
        return [grad.astype(jnp.bfloat16).reshape(parts, -1, grad.shape[1]) for grad in grads]

    grad_qkv_rows, diagonals, squares, down_grad = attention_back(
        lengths,
        qkv_rows,
        grad_attended,
        bias_rows(position_bias.T, seq_len, -1),
        seq_len,
        blocks(grad_down),
        early_pieces(model_width),
        5,
    )
    bias_grad_local = bias_gradient(diagonals, seq_len, bucket_count)
    grad_qkv = lax.dot_general(
        normed_one, grad_qkv_rows, CONTRACT_ROWS, preferred_element_type=jnp.float32
    )
    grad_normed_one = lax.dot_general(
        grad_qkv_rows, qkv_back, CONTRACT_COLS, preferred_element_type=jnp.float32
    )
    grad_emb_part, gain_one = rms_backward(embedded, inverse_one, norm_gains[0], grad_normed_one)
    grad_embedded = grad_residual + grad_emb_part
    table_grad, square_part, qkv_grad, out_grad, in_grad = back(
        grad_embedded.astype(jnp.bfloat16),
        slot_keys,
        asked_rows.reshape(1, -1),
        squares,
        blocks(grad_qkv, grad_out, grad_in),
        late_pieces([grad.shape[1] for grad in (grad_qkv, grad_out, grad_in)]),
        embed_table.shape[0],
        model_width // 128,
        2,
    )
    weight_grads = (qkv_grad, out_grad, in_grad, down_grad)
    total = small_total(
        [gain.reshape(1, -1) for gain in (gain_one, gain_two, gain_three)],
        bias_grad_local,
        square_part,
        4,
    )
    norm_cell, loss_cell, *updated = update(
        total,
        loss_cell,
        table_grad,
        (embed_table, embed_first, embed_second),
        (
            norm_gains,
            gains_first,
            gains_second,
            position_bias.T,
            bias_first.T,
            bias_second.T,
        ),
        weight_grads,
        (
            (qkv_weight, qkv_first, qkv_second),
            (out_weight, out_first, out_second),
            (in_weight, in_first, in_second),
            (down_weight, down_first, down_second),
        ),
    )
    return (loss_cell[0, 0], norm_cell[0, 0], *updated[:3], *updated[9:], *updated[3:6], *(new.T for new in updated[6:9]))


def local(*arrays):
    n_dp, n_pair = lax.axis_size("dp"), lax.axis_size("pair")
    lengths, qkv_weight, down_weight = arrays[2], arrays[9], arrays[18]
    fits = (
        n_pair == 4
        and n_dp & (n_dp - 1) == 0
        and qkv_weight.shape[0] % 8 == 0
        and down_weight.shape[0] % 8 == 0
        and lengths.shape[0] == 2
        and 2 * arrays[1].size // n_dp % 128 == 0
    )
    return (local_fast if fits else local_plain)(*arrays)


def solution(mesh):
    return jax.shard_map(
        local,
        mesh=mesh,
        in_specs=(
            P(("dp", "pair"), None, None),
            P(("dp", "pair"), None),
            P(("dp", "pair")),
            P(),
            P(),
            P(),
            P("dp", None),
            P("dp", None),
            P("dp", None),
            P(("dp", "pair"), None),
            P(("dp", "pair"), None),
            P(("dp", "pair"), None),
            P(("dp", "pair"), None),
            P(("dp", "pair"), None),
            P(("dp", "pair"), None),
            P(("dp", "pair"), None),
            P(("dp", "pair"), None),
            P(("dp", "pair"), None),
            P(("dp", "pair"), None),
            P(("dp", "pair"), None),
            P(("dp", "pair"), None),
            P(),
            P(),
            P(),
            P(),
            P(),
            P(),
        ),
        out_specs=(
            P(),
            P(),
            P("dp", None),
            P("dp", None),
            P("dp", None),
            P(("dp", "pair"), None),
            P(("dp", "pair"), None),
            P(("dp", "pair"), None),
            P(("dp", "pair"), None),
            P(("dp", "pair"), None),
            P(("dp", "pair"), None),
            P(("dp", "pair"), None),
            P(("dp", "pair"), None),
            P(("dp", "pair"), None),
            P(("dp", "pair"), None),
            P(("dp", "pair"), None),
            P(("dp", "pair"), None),
            P(),
            P(),
            P(),
            P(),
            P(),
            P(),
        ),
        check_vma=False,
    )
```

profile of v0, /device:TPU:0, one launch (start us, length us, event | category | flops | bytes accessed | tf_op | source)
XLA Modules:
  0.0 480.2 jit_solution(2426127247246414141)
XLA Ops:
  5.9 1.7 convolution_bitcast_fusion.1.w_ref
  7.6 1.7 convolution_bitcast_fusion.refs_5_
  9.3 118.1 %rows_and_weights.1 = (bf16[1024,768]{1,0:T(8,128)(2,1)}, s32[1,1024]{1,0:T(1,128)}, s32[8,1,256]{2,1,0:T(1,128)}, bf16[32,24,2304]{2,1,0:T(8,128)(2,1)}, bf16[3...) custom-call(s32[1,1024]{1,0:T(1,128)} %bitcast.90, s32[1,1024]{1,0:T(1,128)} %bitcast.86, ...), custom_call_target="tpu_custom_call" | custom-call | tf_op jit(solution)/shard_map/rows_and_weights/pallas_call | solution.py:633
  127.4 1.8 fusion.11
  129.8 8.8 %convolution_convert_fusion.q_ref.k_ref.v_ref.refs_1_.refs_2_.refs_3_ = bf16[1024,2304]{1,0:T(8,128)(2,1)} fusion(bf16[768,2304]{1,0:T(8,128)(2,1)} %bitcast.105, bf16[1024,768]{1,0:T(8,128)(2,1)} %get-tuple-element.64, f32[768]{0:T(1024)} %get-tuple-element.113, f32[1024]{0:T(1024)S(1)} %add_rsqrt_fusion.2), kind=kOutput, calls=%fused_computation.2 | convolution fusion | flops 3629383680 | bytes 9837568 | tf_op jit(solution)/shard_map/dot_general | solution.py:1659
  138.6 21.5 %attention.1 = bf16[1024,768]{1,0:T(8,128)(2,1)S(1)} custom-call(s32[2]{0:T(128)S(1)} %copy-done.1, bf16[1024,2304]{1,0:T(8,128)(2,1)} %convolution_convert_fusion.q_ref.k_ref.v_ref.refs_1_.refs_2_.refs_3_, bf16[1024,2304]{1,0:T(8,128)(2,1)} %convolution_convert_fusion.q_ref.k_ref.v_ref.refs_1_.refs_2_.refs_3_, ...), custom_call_target="tpu_custom_call" | custom-call | tf_op jit(solution)/shard_map/attention/pallas_call | solution.py:327
  161.8 5.8 %maximum_convert_fusion = bf16[1024,3072]{1,0:T(8,128)(2,1)S(1)} fusion(bf16[768,3072]{1,0:T(8,128)(2,1)S(1)} %bitcast.97, f32[1024,768]{1,0:T(8,128)S(1)} %get-tuple-element.115, f32[768]{0:T(1024)S(1)} %copy-done.17, f32[1024]{0:T(1024)S(1)} %add_rsqrt_fusion.1), kind=kOutput, calls=%fused_computation.1 | convolution fusion | flops 4840488960 | bytes 14162944 | tf_op jit(solution)/shard_map/dot_general | solution.py:1666
  167.7 5.3 %multiply_reduce_fusion.2 = (f32[1024]{0:T(1024)S(1)}, f32[1024,768]{1,0:T(8,128)S(1)}) fusion(f32[1024,768]{1,0:T(8,128)S(1)} %get-tuple-element.115, bf16[1024,3072]{1,0:T(8,128)(2,1)S(1)} %maximum_convert_fusion, bf16[3072,768]{1,0:T(8,128)(2,1)S(1)} %bitcast.104), kind=kOutput, calls=%fused_computation.34 | convolution fusion | flops 4834196480 | bytes 17305600 | tf_op jit(solution)/shard_map/dot_general | solution.py:1669
  175.8 14.7 %pooled_loss.1 = (f32[1,1]{1,0:T(1,128)}, f32[2,768]{1,0:T(2,128)}) custom-call(f32[2,768]{1,0:T(2,128)} %broadcast_divide_fusion.1.x_ref, s32[1,64]{1,0:T(1,128)} %bitcast.93, s32[7,64]{1,0:T(8,128)} %bitcast.92, s32[1,64]{1,0:T(1,128)} %bitcast.94), custom_call_target="tpu_custom_call" | custom-call | tf_op jit(solution)/shard_map/pooled_loss/pallas_call | solution.py:267
  191.5 3.2 fusion.18
  196.3 8.9 %select_convert_fusion = bf16[1024,3072]{1,0:T(8,128)(2,1)S(1)} fusion(bf16[1024,3072]{1,0:T(8,128)(2,1)} %copy-done.21, bf16[1024,768]{1,0:T(8,128)(2,1)S(1)} %fusion.19, bf16[3072,768]{1,0:T(8,128)(2,1)} %bitcast.101), kind=kOutput, calls=%fused_computation | convolution fusion | flops 4841275392 | bytes 18874368 | tf_op jit(solution)/shard_map/dot_general | solution.py:1691
  205.2 9.8 %convolution_convert_fusion.2 = bf16[3072,768]{1,0:T(8,128)(2,1)} fusion(bf16[1024,3072]{1,0:T(8,128)(2,1)} %copy-done.21, bf16[1024,768]{1,0:T(8,128)(2,1)S(1)} %fusion.19), kind=kOutput, calls=%fused_computation.4 | convolution fusion | flops 4834197504 | bytes 12582912 | tf_op jit(solution)/shard_map/dot_general | solution.py:1688
  215.0 5.5 %multiply_reduce_fusion = (f32[768]{0:T(1024)S(1)}, f32[1024]{0:T(1024)S(1)}, f32[1024,768]{1,0:T(8,128)S(1)}) fusion(f32[1024,768]{1,0:T(8,128)S(1)} %copy-done.9, f32[1024]{0:T(1024)S(1)} %add_rsqrt_fusion.1, f32[768]{0:T(1024)S(1)} %copy-done.17, bf16[1024,3072]{1,0:T(8,128)(2,1)S(1)} %select_convert_fusion, bf16[768,3072]{1,0:T(8,128)(2,1)S(1)} %bitcast.100), kind=kOutput, calls=%fused_computation.30 | convolution fusion | flops 4836554752 | bytes 17315840 | tf_op jit(solution)/shard_map/dot_general | solution.py:1698
  220.5 7.2 %convolution_convert_fusion.1 = bf16[768,3072]{1,0:T(8,128)(2,1)} fusion(bf16[1024,3072]{1,0:T(8,128)(2,1)S(1)} %select_convert_fusion, f32[1024,768]{1,0:T(8,128)S(1)} %copy-done.9, f32[768]{0:T(1024)S(1)} %copy-done.17, f32[1024]{0:T(1024)S(1)} %add_rsqrt_fusion.1), kind=kOutput, calls=%fused_computation.3 | convolution fusion | flops 4836556800 | bytes 14162944 | tf_op jit(solution)/shard_map/dot_general | solution.py:1695
  228.3 1.8 multiply_add_fusion
  230.2 2.5 convolution_convert_fusion.5
  232.7 2.7 convolution_convert_fusion.4.refs_4_
  235.4 52.1 %attention_back.1 = (bf16[1024,2304]{1,0:T(8,128)(2,1)}, f32[6,2,8,256]{3,2,1,0:T(8,128)}, f32[1,1]{1,0:T(1,128)}, f32[96,768]{1,0:T(8,128)}) custom-call(s32[2]{0:T(128)} %refs_0_.1, bf16[1024,2304]{1,0:T(8,128)(2,1)} %convolution_convert_fusion.q_ref.k_ref.v_ref.refs_1_.refs_2_.refs_3_, ...), custom_call_target="tpu_custom_call" | custom-call | tf_op jit(solution)/shard_map/attention_back/pallas_call | solution.py:920
  287.5 8.2 %fusion.6 = (f32[1024]{0:T(1024)S(1)}, f32[768]{0:T(1024)S(1)}, f32[1024,768]{1,0:T(8,128)S(1)}) fusion(bf16[1024,768]{1,0:T(8,128)(2,1)} %get-tuple-element.64, f32[768]{0:T(1024)} %get-tuple-element.113, f32[1024]{0:T(1024)} %copy-done.14, bf16[1024,2304]{1,0:T(8,128)(2,1)} %get-tuple-element.70, bf16[768,2304]{1,0:T(8,128)(2,1)} %bitcast.106), kind=kOutput, calls=%fused_computation.15 | convolution fusion | flops 3629381888 | bytes 12990464 | tf_op jit(solution)/shard_map/dot_general | solution.py:1729
  295.8 2.0 fusion.10.refs_0_
  299.7 5.6 %convolution_convert_fusion.3 = bf16[768,2304]{1,0:T(8,128)(2,1)} fusion(bf16[1024,2304]{1,0:T(8,128)(2,1)S(1)} %copy-done.19, bf16[1024,768]{1,0:T(8,128)(2,1)S(1)} %copy-done.7, f32[768]{0:T(1024)S(1)} %copy-done.16, f32[1024]{0:T(1024)S(1)} %copy-done.15), kind=kOutput, calls=%fused_computation.5 | convolution fusion | flops 3628793856 | bytes 9837568 | tf_op jit(solution)/shard_map/dot_general | solution.py:1726
  305.3 129.2 %table_and_weights.1 = (bf16[4096,768]{1,0:T(8,128)(2,1)}, f32[1,1]{1,0:T(1,128)}, f32[24,2304]{1,0:T(8,128)}, f32[24,768]{1,0:T(8,128)}, f32[24,3072]{1,0:T(8,128)}) custom-call(bf16[1024,768]{1,0:T(8,128)(2,1)} %fusion.10.refs_0_, s32[1,1024]{1,0:T(1,128)} %get-tuple-element.72.refs_1_, s32[1,2048]{1,0:T(1,128)} %bitcast.89, ...), custom_call_target="tpu_custom_call" | custom-call | tf_op jit(solution)/shard_map/table_and_weights/pallas_call | solution.py:1161
  434.6 13.4 %small_total.1.refs_0_ = f32[40,128]{1,0:T(8,128)} custom-call(f32[1,768]{1,0:T(1,128)} %reshape.167.refs_0_, f32[1,768]{1,0:T(1,128)} %reshape.168.refs_1_, f32[1,768]{1,0:T(1,128)} %reshape.169.refs_2_, f32[12,32]{1,0:T(8,128)} %fusion.24.refs_3_, f32[1,1]{1,0:T(1,128)} %get-tuple-element.75.refs_4_), custom_call_target="tpu_custom_call" | custom-call | tf_op jit(solution)/shard_map/small_total/pallas_call | solution.py:1241
  447.9 31.8 %update.1 = (f32[1,1]{1,0:T(1,128)}, f32[1,1]{1,0:T(1,128)}, f32[4016,768]{1,0:T(8,128)}, f32[4016,768]{1,0:T(8,128)}, f32[4016,768]{1,0:T(8,128)}, /*index=5*/f...) custom-call(f32[40,128]{1,0:T(8,128)} %small_total.1.refs_0_, ...), custom_call_target="tpu_custom_call" | custom-call | tf_op jit(solution)/shard_map/update/pallas_call | solution.py:1323
  (81 shorter events, 15.2 us)
Async XLA Ops:
  129.8 8.8 %copy-start = (f32[12,1024]{1,0:T(8,128)S(1)}, f32[12,1024]{1,0:T(8,128)}, u32[]{:S(2)}) copy-start(f32[12,1024]{1,0:T(8,128)} %convolution_bitcast_fusion.1.w_ref) | copy-start | bytes 147460
  129.8 8.8 %copy-start.1 = (s32[2]{0:T(128)S(1)}, s32[2]{0:T(128)}, u32[]{:S(2)}) copy-start(s32[2]{0:T(128)} %refs_0_.1) | copy-start | bytes 28
  129.8 31.9 %slice-start = ((s8[4718592]{0:T(1024)(128)(4,1)}), s8[4194304]{0:T(1024)(128)(4,1)S(1)}, s32[]{:S(2)}) async-start(s8[4718592]{0:T(1024)(128)(4,1)} %bitcast.95), calls=%async_computation | async-start | bytes 8388608
  138.6 21.5 %copy-start.6 = (bf16[1024,768]{1,0:T(8,128)(2,1)S(1)}, bf16[1024,768]{1,0:T(8,128)(2,1)}, u32[]{:S(2)}) copy-start(bf16[1024,768]{1,0:T(8,128)(2,1)} %get-tuple-element.64) | copy-start | bytes 4718596
  138.6 21.6 %copy-start.20 = (bf16[32,24,768]{2,1,0:T(8,128)(2,1)S(1)}, bf16[32,24,768]{2,1,0:T(8,128)(2,1)}, u32[]{:S(2)}) copy-start(bf16[32,24,768]{2,1,0:T(8,128)(2,1)} %get-tuple-element.66) | copy-start | bytes 3538948
  138.6 23.1 %slice-start.1 = ((s8[4718592]{0:T(1024)(128)(4,1)}), s8[524288]{0:T(1024)(128)(4,1)S(1)}, s32[]{:S(2)}) async-start(s8[4718592]{0:T(1024)(128)(4,1)} %bitcast.95), calls=%async_computation.1 | async-start | bytes 1048576
  160.2 7.5 %slice-start.4 = ((s8[4718592]{0:T(1024)(128)(4,1)}), s8[4194304]{0:T(1024)(128)(4,1)S(1)}, s32[]{:S(2)}) async-start(s8[4718592]{0:T(1024)(128)(4,1)} %bitcast.102), calls=%async_computation.4 | async-start | bytes 8388608
  161.7 5.9 %copy-start.8 = (f32[1024,768]{1,0:T(8,128)}, f32[1024,768]{1,0:T(8,128)S(1)}, u32[]{:S(2)}) copy-start(f32[1024,768]{1,0:T(8,128)S(1)} %get-tuple-element.115) | copy-start | bytes 9437188
  161.8 5.9 %slice-start.5 = ((s8[4718592]{0:T(1024)(128)(4,1)}), s8[524288]{0:T(1024)(128)(4,1)S(1)}, s32[]{:S(2)}) async-start(s8[4718592]{0:T(1024)(128)(4,1)} %bitcast.102), calls=%async_computation.5 | async-start | bytes 1048576
  167.7 5.3 %copy-start.21 = (bf16[1024,3072]{1,0:T(8,128)(2,1)}, bf16[1024,3072]{1,0:T(8,128)(2,1)S(1)}, u32[]{:S(2)}) copy-start(bf16[1024,3072]{1,0:T(8,128)(2,1)S(1)} %maximum_convert_fusion) | copy-start | bytes 18874372
  167.7 7.0 %copy-start.11 = (f32[768]{0:T(1024)S(1)}, f32[768]{0:T(1024)}, u32[]{:S(2)}) copy-start(f32[768]{0:T(1024)} %get-tuple-element.111) | copy-start | bytes 9220
  167.7 7.0 %copy-start.13 = (pred[1024]{0:T(1024)(128)(4,1)S(1)}, pred[1024]{0:T(1024)(128)(4,1)}, u32[]{:S(2)}) copy-start(pred[1024]{0:T(1024)(128)(4,1)} %lt.23) | copy-start | bytes 3076
  190.6 4.7 copy-start.3
  195.2 19.8 %slice-start.2 = ((s8[4718592]{0:T(1024)(128)(4,1)}), s8[4194304]{0:T(1024)(128)(4,1)S(1)}, s32[]{:S(2)}) async-start(s8[4718592]{0:T(1024)(128)(4,1)} %bitcast.98), calls=%async_computation.2 | async-start | bytes 8388608
  196.2 18.8 %slice-start.3 = ((s8[4718592]{0:T(1024)(128)(4,1)}), s8[524288]{0:T(1024)(128)(4,1)S(1)}, s32[]{:S(2)}) async-start(s8[4718592]{0:T(1024)(128)(4,1)} %bitcast.98), calls=%async_computation.3 | async-start | bytes 1048576
  205.2 9.8 %copy-start.9 = (f32[1024,768]{1,0:T(8,128)S(1)}, f32[1024,768]{1,0:T(8,128)}, u32[]{:S(2)}) copy-start(f32[1024,768]{1,0:T(8,128)} %copy-done.8) | copy-start | bytes 9437188
  230.1 2.5 copy-start.4
  287.5 8.2 %copy-start.5 = (f32[1024,768]{1,0:T(8,128)S(1)}, f32[1024,768]{1,0:T(8,128)}, u32[]{:S(2)}) copy-start(f32[1024,768]{1,0:T(8,128)} %copy-done.4) | copy-start | bytes 9437188
  287.5 8.2 %copy-start.7 = (bf16[1024,768]{1,0:T(8,128)(2,1)S(1)}, bf16[1024,768]{1,0:T(8,128)(2,1)}, u32[]{:S(2)}) copy-start(bf16[1024,768]{1,0:T(8,128)(2,1)} %get-tuple-element.64) | copy-start | bytes 4718596
  287.5 8.2 %copy-start.15 = (f32[1024]{0:T(1024)S(1)}, f32[1024]{0:T(1024)}, u32[]{:S(2)}) copy-start(f32[1024]{0:T(1024)} %copy-done.14) | copy-start | bytes 12292
  287.5 8.2 %copy-start.16 = (f32[768]{0:T(1024)S(1)}, f32[768]{0:T(1024)}, u32[]{:S(2)}) copy-start(f32[768]{0:T(1024)} %get-tuple-element.113) | copy-start | bytes 9220
  295.8 2.6 copy-start.12
  295.8 2.7 copy-start.10
  295.8 3.9 copy-start.19
  (4 other events, 6.0 us)
where the time goes:
time: 489 us; the launch traced here: 480 us
  Pallas kernels  381 us (78%)
  matrix products  76.5 us (16%)
  other arithmetic  13.8 us (3%)
  local copies, waits for them, and re-layouts  7.45 us (2%)
    pallas_call x1, Pallas kernels, back(): pl.pallas_call(functools.partial(back_kernel, n_dp, n_pair, pieces, len(g...  129 us
    pallas_call x1, Pallas kernels, front(): pl.pallas_call(functools.partial(front_kernel, n_dp, n_pair, pieces, len(...  118 us
    pallas_call x1, Pallas kernels, attention_back(): pl.pallas_call(functools.partial(backward_kernel, n_dp, n_pair, pieces, l...  52.1 us
    pallas_call x1, Pallas kernels, update(): pl.pallas_call(functools.partial(update_kernel, len(grads)), grid=(steps,...  31.8 us
    pallas_call x1, Pallas kernels, attention(): pl.pallas_call(forward_kernel, grid_spec=pltpu.PrefetchScalarGridSpec(num...  21.5 us
    pallas_call x1, Pallas kernels, pooled_loss(): pl.pallas_call(functools.partial(loss_kernel, n_dp, n_pair), out_shape=[j...  14.7 us
    pallas_call x1, Pallas kernels, small_total(): pl.pallas_call(functools.partial(norm_kernel, n_dp, n_pair, count), out_s...  13.4 us
    dot_general x1, matrix products, local_fast(): lax.dot_general(hidden, grad_branch, CONTRACT_ROWS, preferred_element_typ...  9.81 us

commit v1 on v0

--- a/solution.py
+++ b/solution.py
@@ -286,10 +286,10 @@
 NT = (((1,), (1,)), ((), ()))
 TN = (((0,), (0,)), ((), ()))
 
-def band(w_ref, row, h, table, seq):
+def band(w_ref, row, base, h, table, seq):
     tiles = seq // 128
     for d in range(1 - tiles, tiles):
-        low = seq + 128 * d - 128
+        low = base + seq + 128 * d - 128
         x = jnp.broadcast_to(w_ref[pl.ds(row, 1), low : low + 256], (128, 256))
         tile = pltpu.roll(x, 0, 1, stride=1, stride_axis=0)[:, 128:]
         for a in range(tiles):
@@ -302,7 +302,7 @@
     @pl.when(doc == 0)
     def _():
         for h in range(2):
-            band(w_ref, 2 * pl.program_id(0) + h, h, table, seq)
+            band(w_ref, 2 * pl.program_id(0) + h, 0, h, table, seq)
     length = len_ref[doc]
     lane = lax.broadcasted_iota(jnp.int32, (seq, 128), 1)
     column = lax.broadcasted_iota(jnp.int32, (1, seq), 1)
@@ -348,8 +348,9 @@
     return (bucket[:, None] == np.arange(buckets)[None, :]).astype(np.float32)
 
 
-def bias_rows(bias, seq, sign):
-    hits = bucket_hits(sign * (np.arange(2 * seq) - seq), bias.shape[1])
+def bias_rows(bias, seq):
+    offsets = np.arange(2 * seq) - seq
+    hits = bucket_hits(np.concatenate([offsets, -offsets]), bias.shape[1])
     return jnp.dot(bias, hits.T, precision=HIGHEST)
 
 
@@ -375,7 +376,7 @@
 
 
 def early_pieces(width):
-    cut = width * 2 // 3 // 128 * 128
+    cut = width // 2 // 128 * 128
     return [(0, 0, cut, 0), (0, cut, width, 1)]
 
 
@@ -507,8 +508,13 @@
     table_sem, ask_sem, row_sem, *sems = rest[7:]
     dp, pair = lax.axis_index("dp"), lax.axis_index("pair")
     weights = Gather(n_dp, n_pair, pieces, outs, bufs, sems)
-    tokens = owner_ref.shape[1]
+    docs, seq = owner_ref.shape
+    tokens = docs * seq
     cap = ask_out.shape[2]
+
+    def in_line(ref):
+        return jnp.concatenate([ref[d : d + 1, :] for d in range(docs)], axis=1)
+
     table_rows = table_ref.shape[0]
     load = pltpu.make_async_copy(table_ref, wide, table_sem)
     load.start()
@@ -522,7 +528,7 @@
     pl.semaphore_wait(sem, n_dp + 1)
     weights.held(0)
 
-    owner = owner_ref[...]
+    owner = in_line(owner_ref)
     by_owner = lax.broadcasted_iota(jnp.int32, (n_dp, tokens), 0) == owner
     ranks = jnp.dot(
         jnp.where(by_owner, 1.0, 0.0).astype(jnp.bfloat16),
@@ -532,7 +538,7 @@
     rank = jnp.sum(jnp.where(by_owner, ranks, 0.0), axis=0, keepdims=True)
     key = owner * cap + rank.astype(jnp.int32)
     key_ref[...] = key
-    wanted = digits(row_ref[...])
+    wanted = digits(in_line(row_ref))
 
     def peer(j):
         return {"dp": dp ^ j, "pair": pair}
@@ -626,7 +632,7 @@
 def front(owner, row, table, shards, pieces, cap, n_dp, n_pair, cid):
     n, k = n_dp * n_pair, len(pieces)
     hops = (n - 1).bit_length() - 2
-    tokens = owner.shape[1]
+    tokens = owner.size
     table_rows, width = table.shape
     padded = -(-table_rows // 256) * 256
     sem = pltpu.SemaphoreType.DMA
@@ -812,21 +818,21 @@
         for r in reversed(range(hops + 1)):
             weights.core_out(r)
 
-    @pl.when(at == 2)
+    @pl.when(at == 1)
     def _():
         weights.loaded()
         weights.core_in(hops)
 
-    @pl.when(at == 3)
+    @pl.when(at == 2)
     def _():
         for r in reversed(range(hops)):
             weights.core_in(r)
 
-    @pl.when(at == 6)
+    @pl.when(at == 5)
     def _():
         weights.side_in(hops)
 
-    @pl.when(at == 7)
+    @pl.when(at == 6)
     def _():
         for r in reversed(range(hops)):
             weights.side_in(r)
@@ -837,7 +843,7 @@
     @pl.when(doc == 0)
     def _():
         for h in range(2):
-            band(w_ref, 2 * pl.program_id(0) + h, h, table, seq)
+            band(w_ref, 2 * pl.program_id(0) + h, 2 * seq, h, table, seq)
         total[...] = jnp.zeros_like(total)
     length = len_ref[doc]
     lane = lax.broadcasted_iota(jnp.int32, (seq, 128), 1)
@@ -877,7 +883,7 @@
         out(i).start()
 
     for r in range(1, hops):
-        @pl.when(step == pairs * docs - 1 - r)
+        @pl.when(step == pairs * docs - 2 * r)
         def _():
             weights.hop_in(r)
 
@@ -955,16 +961,22 @@
     )(lengths, qkv, qkv, qkv, g, w, *grads)
 
 
-def back_kernel(n_dp, n_pair, pieces, n_in, chunk, *refs):
+def packed_base(gains, width):
+    return -(-gains * width // 128 // 8) * 8
+
+
+def back_kernel(n_dp, n_pair, pieces, n_gain, n_in, chunk, *refs):
     k = len(pieces)
-    grad_ref, key_ref, ask_ref, squares_ref = refs[:4]
-    ins = refs[4 : 4 + n_in]
-    out_ref, square_ref = refs[4 + n_in : 6 + n_in]
-    outs = refs[6 + n_in : 6 + 2 * n_in]
-    rest = refs[6 + 2 * n_in :]
+    grad_ref, key_ref, ask_ref, squares_ref, bias_ref = refs[:5]
+    gain_refs = refs[5 : 5 + n_gain]
+    ins, rest = refs[5 + n_gain : 5 + n_gain + n_in], refs[5 + n_gain + n_in :]
+    out_ref, total_ref = rest[:2]
+    outs = rest[2 : 2 + n_in]
+    rest = rest[2 + n_in :]
     boxes, rest = rest[: 4 * k], rest[4 * k :]
     rows_out, rows_in, hot, part, stage_out, got_core, out_side, got_side, other = rest[:9]
-    row_sem, core_sem, side_sem, last_sem, out_sem, *sems = rest[9:]
+    square_ref, small, by_dp, from_pair = rest[9:13]
+    row_sem, core_sem, side_sem, last_sem, out_sem, dp_sem, pair_sem, *sems = rest[13:]
     dp, pair = lax.axis_index("dp"), lax.axis_index("pair")
     core = lax.rem(pair, 2)
     weights = Scatter(n_dp, n_pair, pieces, ins, outs, boxes, sems)
@@ -1115,8 +1127,54 @@
     for ref in outs:
         square = jnp.sum(ref[...] * ref[...], axis=0, keepdims=True)
         square_ref[...] += jnp.sum(square, axis=1, keepdims=True)
+    gains_width = gain_refs[0].shape[1]
+    base = packed_base(n_gain, gains_width)
+    small[...] = jnp.zeros_like(small)
+    for c in range(gains_width // 128):
+        for which in range(n_gain):
+            at = c * n_gain + which
+            small[0, at : at + 1, :] = gain_refs[which][:, c * 128 : (c + 1) * 128]
+    small[0, base : base + bias_ref.shape[0], : bias_ref.shape[1]] = bias_ref[...]
+    small[0, base : base + 1, 127:128] = square_ref[...]
+
+    def to_dp(j, slot):
+        return remote(
+            small.at[0],
+            by_dp.at[slot],
+            dp_sem.at[0, j],
+            dp_sem.at[1, j],
+            {"dp": dp ^ j, "pair": pair},
+        )
+
+    def to_pair(turn, target):
+        return remote(
+            small.at[1 + turn],
+            from_pair.at[turn],
+            pair_sem.at[0, turn],
+            pair_sem.at[1, turn],
+            target,
+        )
+
+    for j in far:
+        to_dp(j, dp).start()
+    by_dp[dp] = small[0]
     for g in range(groups):
         hand_over(g)
+    for j in far:
+        to_dp(j, dp ^ j).wait_recv()
+    total = by_dp[0]
+    for d in range(1, n_dp):
+        total = total + by_dp[d]
+    for turn, target in enumerate((partner, across)):
+        small[1 + turn] = total
+        to_pair(turn, target).start()
+        to_pair(turn, target).wait_recv()
+        total = total + from_pair[turn]
+    total_ref[...] = total
+    for j in far:
+        to_dp(j, dp).wait_send()
+    for turn, target in enumerate((partner, across)):
+        to_pair(turn, target).wait_send()
     for g in range(groups):
         for j in far:
             row(g, j).wait_send()
@@ -1145,7 +1203,7 @@
     ]
 
 
-def back(grad, key, asked, squares, grads, pieces, table_rows, groups, cid):
+def back(grad, key, asked, squares, bias, gains, grads, pieces, table_rows, groups, cid):
     n_dp, n_pair = lax.axis_size("dp"), lax.axis_size("pair")
     boxes, sems = scatter_scratch(n_dp * n_pair, grads, pieces)
     chunk = 512
@@ -1154,18 +1212,19 @@
     tokens, full = grad.shape
     width = full // groups
     slots = asked.shape[1]
+    height = -(-(packed_base(len(gains), full) + bias.shape[0]) // 8) * 8
     cap = slots // n_dp
     sem = pltpu.SemaphoreType.DMA
     box = pltpu.VMEM((groups, count, chunk, width), jnp.bfloat16)
 
     return pl.pallas_call(
-        functools.partial(back_kernel, n_dp, n_pair, pieces, len(grads), chunk),
+        functools.partial(back_kernel, n_dp, n_pair, pieces, len(gains), len(grads), chunk),
         out_shape=[
             jax.ShapeDtypeStruct((rows, full), jnp.bfloat16),
-            jax.ShapeDtypeStruct((1, 1), jnp.float32),
+            jax.ShapeDtypeStruct((height, 128), jnp.float32),
         ]
         + [jax.ShapeDtypeStruct(g.shape[1:], jnp.float32) for g in grads],
-        in_specs=[VM] * 4 + [ANY] * len(grads),
+        in_specs=[VM] * (5 + len(gains)) + [ANY] * len(grads),
         out_specs=[ANY, VM] + [VM] * len(grads),
         scratch_shapes=boxes
         + [
@@ -1178,18 +1237,24 @@
             box,
             box,
             box,
+            pltpu.VMEM((1, 1), jnp.float32),
+            pltpu.VMEM((3, height, 128), jnp.float32),
+            pltpu.VMEM((n_dp, height, 128), jnp.float32),
+            pltpu.VMEM((2, height, 128), jnp.float32),
             sem((2, groups, n_dp)),
             sem((2, groups, count)),
             sem((2, groups, count)),
             sem((2, groups, count)),
             sem((groups, count)),
+            sem((2, n_dp)),
+            sem((2, 2)),
         ]
         + sems,
         compiler_params=pltpu.CompilerParams(
             collective_id=cid, has_side_effects=True, vmem_limit_bytes=VMEM_LIMIT
         ),
         name="table_and_weights",
-    )(grad, key, asked, squares, *grads)
+    )(grad, key, asked, squares, bias, *gains, *grads)
 
 
 BIAS_CORRECT = (1.0 - beta_one**STEP, 1.0 - beta_two**STEP)
@@ -1202,56 +1267,6 @@
     root = jnp.sqrt(second_new * (1.0 / BIAS_CORRECT[1])) + adam_eps
     step = (rate / BIAS_CORRECT[0]) * first_new / root
     return (weight * (1.0 - rate * shrink) - step, first_new, second_new)
-
-
-def packed_base(gains, width):
-    return -(-gains * width // 128 // 8) * 8
-
-
-def norm_kernel(n_dp, n_pair, n_gain, *refs):
-    gain_refs = refs[:n_gain]
-    bias_ref, square_ref, total_ref, block, by_dp, by_pair = refs[n_gain : n_gain + 6]
-    rounds = Rounds(n_dp, n_pair, *refs[n_gain + 6 :])
-    width = gain_refs[0].shape[1]
-    base = packed_base(n_gain, width)
-    block[...] = jnp.zeros_like(block)
-    for c in range(width // 128):
-        for g in range(n_gain):
-            at = c * n_gain + g
-            block[at : at + 1, :] = gain_refs[g][:, c * 128 : (c + 1) * 128]
-    block[base : base + bias_ref.shape[0], : bias_ref.shape[1]] = bias_ref[...]
-    block[base : base + 1, 127:128] = square_ref[...]
-    rounds.entered()
-    rounds.over_dp(block, by_dp)
-    total = by_dp[0]
-    for d in range(1, n_dp):
-        total = total + by_dp[d]
-    block[...] = total
-    rounds.over_pair(block, by_pair)
-    total = by_pair[0]
-    for p in range(1, n_pair):
-        total = total + by_pair[p]
-    total_ref[...] = total
-
-
-def small_total(gain_grads, bias_grad, square, cid):
-    n_dp, n_pair = lax.axis_size("dp"), lax.axis_size("pair")
-    count, width = len(gain_grads), gain_grads[0].shape[1]
-    height = -(-(packed_base(count, width) + bias_grad.shape[0]) // 8) * 8
-    return pl.pallas_call(
-        functools.partial(norm_kernel, n_dp, n_pair, count),
-        out_shape=jax.ShapeDtypeStruct((height, 128), jnp.float32),
-        in_specs=[VM] * (count + 2),
-        out_specs=VM,
-        scratch_shapes=[
-            pltpu.VMEM((height, 128), jnp.float32),
-            pltpu.VMEM((n_dp, height, 128), jnp.float32),
-            pltpu.VMEM((n_pair, height, 128), jnp.float32),
-        ]
-        + round_sems(n_dp, n_pair),
-        compiler_params=pltpu.CompilerParams(collective_id=cid, has_side_effects=True),
-        name="small_total",
-    )(*gain_grads, bias_grad, square)
 
 
 def update_kernel(mats, *refs):
@@ -1638,8 +1653,8 @@
     holders = lax.axis_size("pair")
     shards = (qkv_weight, out_weight, in_weight, down_weight)
     embedded_low, slot_keys, asked_rows, *full = front(
-        token_owner.reshape(1, -1),
-        token_row.reshape(1, -1),
+        token_owner.reshape(token_row.shape),
+        token_row,
         embed_table,
         shards,
         weight_pieces([shard.shape[1] for shard in shards]),
@@ -1654,12 +1669,13 @@
     embedded = embedded_low.astype(jnp.float32)
     positions = jnp.arange(seq_len)
     live = positions[None, :] < lengths[:, None]
+    offset_bias = bias_rows(position_bias.T, seq_len)
     normed_one, inverse_one = rms_forward(embedded, norm_gains[0])
     normed_one = normed_one.astype(jnp.bfloat16)
     qkv_rows = jnp.dot(normed_one, qkv_full, preferred_element_type=jnp.float32).astype(
         jnp.bfloat16
     )
-    attended = attention(lengths, qkv_rows, bias_rows(position_bias.T, seq_len, 1), seq_len)
+    attended = attention(lengths, qkv_rows, offset_bias, seq_len)
     residual = embedded + jnp.dot(attended, out_full, preferred_element_type=jnp.float32)
     normed_two, inverse_two = rms_forward(residual, norm_gains[1])
     normed_two = normed_two.astype(jnp.bfloat16)
@@ -1716,7 +1732,7 @@
         lengths,
         qkv_rows,
         grad_attended,
-        bias_rows(position_bias.T, seq_len, -1),
+        offset_bias,
         seq_len,
         blocks(grad_down),
         early_pieces(model_width),
@@ -1731,11 +1747,13 @@
     )
     grad_emb_part, gain_one = rms_backward(embedded, inverse_one, norm_gains[0], grad_normed_one)
     grad_embedded = grad_residual + grad_emb_part
-    table_grad, square_part, qkv_grad, out_grad, in_grad = back(
+    table_grad, total, qkv_grad, out_grad, in_grad = back(
         grad_embedded.astype(jnp.bfloat16),
         slot_keys,
         asked_rows.reshape(1, -1),
         squares,
+        bias_grad_local,
+        [gain.reshape(1, -1) for gain in (gain_one, gain_two, gain_three)],
         blocks(grad_qkv, grad_out, grad_in),
         late_pieces([grad.shape[1] for grad in (grad_qkv, grad_out, grad_in)]),
         embed_table.shape[0],
@@ -1743,12 +1761,6 @@
         2,
     )
     weight_grads = (qkv_grad, out_grad, in_grad, down_grad)
-    total = small_total(
-        [gain.reshape(1, -1) for gain in (gain_one, gain_two, gain_three)],
-        bias_grad_local,
-        square_part,
-        4,
-    )
     norm_cell, loss_cell, *updated = update(
         total,
         loss_cell,

time: 489 us -> 478 us (0.978)
  Pallas kernels: 381 us -> 370 us
    pallas_call x1 -> x0, Pallas kernels: 13.4 us -> none  [small_total(): pl.pallas_call(functools.partial(norm_kernel, n_dp, n_pair, count), out_s...]
where the time goes in v1:
time: 478 us; the launch traced here: 468 us
  Pallas kernels  370 us (77%)
  matrix products  75 us (16%)
  other arithmetic  13.8 us (3%)
  local copies, waits for them, and re-layouts  8.32 us (2%)
    pallas_call x1, Pallas kernels, back(): pl.pallas_call(functools.partial(back_kernel, n_dp, n_pair, pieces, len(g...  133 us
    pallas_call x1, Pallas kernels, front(): pl.pallas_call(functools.partial(front_kernel, n_dp, n_pair, pieces, len(...  118 us
    pallas_call x1, Pallas kernels, attention_back(): pl.pallas_call(functools.partial(backward_kernel, n_dp, n_pair, pieces, l...  50.2 us
    pallas_call x1, Pallas kernels, update(): pl.pallas_call(functools.partial(update_kernel, len(grads)), grid=(steps,...  31.8 us
    pallas_call x1, Pallas kernels, attention(): pl.pallas_call(forward_kernel, grid_spec=pltpu.PrefetchScalarGridSpec(num...  21.5 us
    pallas_call x1, Pallas kernels, pooled_loss(): pl.pallas_call(functools.partial(loss_kernel, n_dp, n_pair), out_shape=[j...  14.7 us
    dot_general x1, matrix products, local_fast(): lax.dot_general(hidden, grad_branch, CONTRACT_ROWS, preferred_element_typ...  9.81 us

profile of v1, /device:TPU:0, one launch (start us, length us, event | category | flops | bytes accessed | tf_op | source)
XLA Modules:
  0.0 468.4 jit_solution(17311657618012962458)
XLA Ops:
  5.9 1.9 convolution_bitcast_fusion.w_ref.refs_5_
  7.8 118.1 %rows_and_weights.1 = (bf16[1024,768]{1,0:T(8,128)(2,1)}, s32[1,1024]{1,0:T(1,128)}, s32[8,1,256]{2,1,0:T(1,128)}, bf16[32,24,2304]{2,1,0:T(8,128)(2,1)}, bf16[3...) custom-call(s32[2,512]{1,0:T(2,128)} %bitcast.81, s32[2,512]{1,0:T(2,128)} %refs_1_.1, ...), custom_call_target="tpu_custom_call" | custom-call | tf_op jit(solution)/shard_map/rows_and_weights/pallas_call | solution.py:639
  125.8 1.8 fusion.11
  128.2 8.8 %convolution_convert_fusion.q_ref.k_ref.v_ref.refs_1_.refs_2_.refs_3_ = bf16[1024,2304]{1,0:T(8,128)(2,1)} fusion(bf16[768,2304]{1,0:T(8,128)(2,1)} %bitcast.98, bf16[1024,768]{1,0:T(8,128)(2,1)} %get-tuple-element.64, f32[768]{0:T(1024)} %get-tuple-element.113, f32[1024]{0:T(1024)S(1)} %add_rsqrt_fusion.2), kind=kOutput, calls=%fused_computation.2 | convolution fusion | flops 3629383680 | bytes 9837568 | tf_op jit(solution)/shard_map/dot_general | solution.py:1675
  137.0 21.5 %attention.1 = bf16[1024,768]{1,0:T(8,128)(2,1)S(1)} custom-call(s32[2]{0:T(128)S(1)} %copy-done.1, bf16[1024,2304]{1,0:T(8,128)(2,1)} %convolution_convert_fusion.q_ref.k_ref.v_ref.refs_1_.refs_2_.refs_3_, bf16[1024,2304]{1,0:T(8,128)(2,1)} %convolution_convert_fusion.q_ref.k_ref.v_ref.refs_1_.refs_2_.refs_3_, ...), custom_call_target="tpu_custom_call" | custom-call | tf_op jit(solution)/shard_map/attention/pallas_call | solution.py:327
  158.6 1.5 multiply_reduce_fusion.3
  160.2 5.8 %maximum_convert_fusion = bf16[1024,3072]{1,0:T(8,128)(2,1)S(1)} fusion(bf16[768,3072]{1,0:T(8,128)(2,1)S(1)} %bitcast.90, f32[1024,768]{1,0:T(8,128)S(1)} %get-tuple-element.115, f32[768]{0:T(1024)S(1)} %copy-done.17, f32[1024]{0:T(1024)S(1)} %add_rsqrt_fusion.1), kind=kOutput, calls=%fused_computation.1 | convolution fusion | flops 4840488960 | bytes 14162944 | tf_op jit(solution)/shard_map/dot_general | solution.py:1682
  166.1 5.3 %multiply_reduce_fusion.2 = (f32[1024]{0:T(1024)S(1)}, f32[1024,768]{1,0:T(8,128)S(1)}) fusion(f32[1024,768]{1,0:T(8,128)S(1)} %get-tuple-element.115, bf16[1024,3072]{1,0:T(8,128)(2,1)S(1)} %maximum_convert_fusion, bf16[3072,768]{1,0:T(8,128)(2,1)S(1)} %bitcast.97), kind=kOutput, calls=%fused_computation.34 | convolution fusion | flops 4834196480 | bytes 17305600 | tf_op jit(solution)/shard_map/dot_general | solution.py:1685
  171.4 1.6 copy-done.2
  174.3 14.7 %pooled_loss.1 = (f32[1,1]{1,0:T(1,128)}, f32[2,768]{1,0:T(2,128)}) custom-call(f32[2,768]{1,0:T(2,128)} %broadcast_divide_fusion.1.x_ref, s32[1,64]{1,0:T(1,128)} %bitcast.86, s32[7,64]{1,0:T(8,128)} %bitcast.85, s32[1,64]{1,0:T(1,128)} %bitcast.87), custom_call_target="tpu_custom_call" | custom-call | tf_op jit(solution)/shard_map/pooled_loss/pallas_call | solution.py:267
  189.9 3.2 fusion.18
  194.7 8.9 %select_convert_fusion = bf16[1024,3072]{1,0:T(8,128)(2,1)S(1)} fusion(bf16[1024,3072]{1,0:T(8,128)(2,1)} %copy-done.21, bf16[1024,768]{1,0:T(8,128)(2,1)S(1)} %fusion.19, bf16[3072,768]{1,0:T(8,128)(2,1)} %bitcast.94), kind=kOutput, calls=%fused_computation | convolution fusion | flops 4841275392 | bytes 18874368 | tf_op jit(solution)/shard_map/dot_general | solution.py:1707
  203.6 9.8 %convolution_convert_fusion.2 = bf16[3072,768]{1,0:T(8,128)(2,1)} fusion(bf16[1024,3072]{1,0:T(8,128)(2,1)} %copy-done.21, bf16[1024,768]{1,0:T(8,128)(2,1)S(1)} %fusion.19), kind=kOutput, calls=%fused_computation.4 | convolution fusion | flops 4834197504 | bytes 12582912 | tf_op jit(solution)/shard_map/dot_general | solution.py:1704
  213.4 5.5 %multiply_reduce_fusion = (f32[768]{0:T(1024)S(1)}, f32[1024]{0:T(1024)S(1)}, f32[1024,768]{1,0:T(8,128)S(1)}) fusion(f32[1024,768]{1,0:T(8,128)S(1)} %copy-done.9, f32[1024]{0:T(1024)S(1)} %add_rsqrt_fusion.1, f32[768]{0:T(1024)S(1)} %copy-done.17, bf16[1024,3072]{1,0:T(8,128)(2,1)S(1)} %select_convert_fusion, bf16[768,3072]{1,0:T(8,128)(2,1)S(1)} %bitcast.93), kind=kOutput, calls=%fused_computation.30 | convolution fusion | flops 4836554752 | bytes 17315840 | tf_op jit(solution)/shard_map/dot_general | solution.py:1714
  218.9 7.2 %convolution_convert_fusion.1 = bf16[768,3072]{1,0:T(8,128)(2,1)} fusion(bf16[1024,3072]{1,0:T(8,128)(2,1)S(1)} %select_convert_fusion, f32[1024,768]{1,0:T(8,128)S(1)} %copy-done.9, f32[768]{0:T(1024)S(1)} %copy-done.17, f32[1024]{0:T(1024)S(1)} %add_rsqrt_fusion.1), kind=kOutput, calls=%fused_computation.3 | convolution fusion | flops 4836556800 | bytes 14162944 | tf_op jit(solution)/shard_map/dot_general | solution.py:1711
  226.7 1.8 multiply_add_fusion
  228.6 2.5 convolution_convert_fusion.5
  231.1 2.7 convolution_convert_fusion.4.refs_4_
  233.8 50.2 %attention_back.1 = (bf16[1024,2304]{1,0:T(8,128)(2,1)}, f32[6,2,8,256]{3,2,1,0:T(8,128)}, f32[1,1]{1,0:T(1,128)}, f32[96,768]{1,0:T(8,128)}) custom-call(s32[2]{0:T(128)} %refs_0_.1, bf16[1024,2304]{1,0:T(8,128)(2,1)} %convolution_convert_fusion.q_ref.k_ref.v_ref.refs_1_.refs_2_.refs_3_, ...), custom_call_target="tpu_custom_call" | custom-call | tf_op jit(solution)/shard_map/attention_back/pallas_call | solution.py:926
  284.0 8.2 %fusion.10 = (f32[768]{0:T(1024)S(1)}, f32[1024]{0:T(1024)S(1)}, f32[1024,768]{1,0:T(8,128)S(1)}) fusion(bf16[1024,768]{1,0:T(8,128)(2,1)} %get-tuple-element.64, f32[1024]{0:T(1024)} %copy-done.14, f32[768]{0:T(1024)} %get-tuple-element.113, bf16[1024,2304]{1,0:T(8,128)(2,1)} %get-tuple-element.70, bf16[768,2304]{1,0:T(8,128)(2,1)} %bitcast.99), kind=kOutput, calls=%fused_computation.19 | convolution fusion | flops 3629381888 | bytes 12990464 | tf_op jit(solution)/shard_map/dot_general | solution.py:1745
  292.8 2.0 fusion.9.refs_0_
  295.7 5.8 %convolution_convert_fusion.3 = bf16[768,2304]{1,0:T(8,128)(2,1)} fusion(bf16[1024,2304]{1,0:T(8,128)(2,1)S(1)} %copy-done.19, bf16[1024,768]{1,0:T(8,128)(2,1)S(1)} %copy-done.7, f32[768]{0:T(1024)S(1)} %copy-done.16, f32[1024]{0:T(1024)S(1)} %copy-done.15), kind=kOutput, calls=%fused_computation.5 | convolution fusion | flops 3628793856 | bytes 9837568 | tf_op jit(solution)/shard_map/dot_general | solution.py:1742
  302.8 133.4 %table_and_weights.1 = (bf16[4096,768]{1,0:T(8,128)(2,1)}, f32[40,128]{1,0:T(8,128)}, f32[24,2304]{1,0:T(8,128)}, f32[24,768]{1,0:T(8,128)}, f32[24,3072]{1,0:T(8,128)}) custom-call(bf16[1024,768]{1,0:T(8,128)(2,1)} %fusion.9.refs_0_, s32[1,1024]{1,0:T(1,128)} %get-tuple-element.71.refs_1_, s32[1,2048]{1,0:T(1,128)} %bitcast.84, ...), custom_call_target="tpu_custom_call" | custom-call | tf_op jit(solution)/shard_map/table_and_weights/pallas_call | solution.py:1220
  436.2 31.8 %update.1 = (f32[1,1]{1,0:T(1,128)}, f32[1,1]{1,0:T(1,128)}, f32[4016,768]{1,0:T(8,128)}, f32[4016,768]{1,0:T(8,128)}, f32[4016,768]{1,0:T(8,128)}, /*index=5*/f...) custom-call(f32[40,128]{1,0:T(8,128)} %get-tuple-element.75.refs_0_,, ...), custom_call_target="tpu_custom_call" | custom-call | tf_op jit(solution)/shard_map/update/pallas_call | solution.py:1338
  (79 shorter events, 13.0 us)
Async XLA Ops:
  128.2 8.8 %copy-start = (f32[12,2048]{1,0:T(8,128)S(1)}, f32[12,2048]{1,0:T(8,128)}, u32[]{:S(2)}) copy-start(f32[12,2048]{1,0:T(8,128)} %convolution_bitcast_fusion.w_ref.refs_5_) | copy-start | bytes 294916
  128.2 8.8 %copy-start.1 = (s32[2]{0:T(128)S(1)}, s32[2]{0:T(128)}, u32[]{:S(2)}) copy-start(s32[2]{0:T(128)} %refs_0_.1) | copy-start | bytes 28
  128.2 31.9 %slice-start = ((s8[4718592]{0:T(1024)(128)(4,1)}), s8[4194304]{0:T(1024)(128)(4,1)S(1)}, s32[]{:S(2)}) async-start(s8[4718592]{0:T(1024)(128)(4,1)} %bitcast.88), calls=%async_computation | async-start | bytes 8388608
  137.0 21.5 %copy-start.6 = (bf16[1024,768]{1,0:T(8,128)(2,1)S(1)}, bf16[1024,768]{1,0:T(8,128)(2,1)}, u32[]{:S(2)}) copy-start(bf16[1024,768]{1,0:T(8,128)(2,1)} %get-tuple-element.64) | copy-start | bytes 4718596
  137.0 21.6 %copy-start.20 = (bf16[32,24,768]{2,1,0:T(8,128)(2,1)S(1)}, bf16[32,24,768]{2,1,0:T(8,128)(2,1)}, u32[]{:S(2)}) copy-start(bf16[32,24,768]{2,1,0:T(8,128)(2,1)} %get-tuple-element.66) | copy-start | bytes 3538948
  137.0 23.1 %slice-start.1 = ((s8[4718592]{0:T(1024)(128)(4,1)}), s8[524288]{0:T(1024)(128)(4,1)S(1)}, s32[]{:S(2)}) async-start(s8[4718592]{0:T(1024)(128)(4,1)} %bitcast.88), calls=%async_computation.1 | async-start | bytes 1048576
  158.6 7.5 %slice-start.4 = ((s8[4718592]{0:T(1024)(128)(4,1)}), s8[4194304]{0:T(1024)(128)(4,1)S(1)}, s32[]{:S(2)}) async-start(s8[4718592]{0:T(1024)(128)(4,1)} %bitcast.95), calls=%async_computation.4 | async-start | bytes 8388608
  160.1 5.9 %copy-start.8 = (f32[1024,768]{1,0:T(8,128)}, f32[1024,768]{1,0:T(8,128)S(1)}, u32[]{:S(2)}) copy-start(f32[1024,768]{1,0:T(8,128)S(1)} %get-tuple-element.115) | copy-start | bytes 9437188
  160.2 5.9 %slice-start.5 = ((s8[4718592]{0:T(1024)(128)(4,1)}), s8[524288]{0:T(1024)(128)(4,1)S(1)}, s32[]{:S(2)}) async-start(s8[4718592]{0:T(1024)(128)(4,1)} %bitcast.95), calls=%async_computation.5 | async-start | bytes 1048576
  166.1 5.3 %copy-start.21 = (bf16[1024,3072]{1,0:T(8,128)(2,1)}, bf16[1024,3072]{1,0:T(8,128)(2,1)S(1)}, u32[]{:S(2)}) copy-start(bf16[1024,3072]{1,0:T(8,128)(2,1)S(1)} %maximum_convert_fusion) | copy-start | bytes 18874372
  166.1 7.0 %copy-start.11 = (f32[768]{0:T(1024)S(1)}, f32[768]{0:T(1024)}, u32[]{:S(2)}) copy-start(f32[768]{0:T(1024)} %get-tuple-element.111) | copy-start | bytes 9220
  166.1 7.0 %copy-start.13 = (pred[1024]{0:T(1024)(128)(4,1)S(1)}, pred[1024]{0:T(1024)(128)(4,1)}, u32[]{:S(2)}) copy-start(pred[1024]{0:T(1024)(128)(4,1)} %lt.23) | copy-start | bytes 3076
  189.0 4.7 copy-start.3
  193.7 19.8 %slice-start.2 = ((s8[4718592]{0:T(1024)(128)(4,1)}), s8[4194304]{0:T(1024)(128)(4,1)S(1)}, s32[]{:S(2)}) async-start(s8[4718592]{0:T(1024)(128)(4,1)} %bitcast.91), calls=%async_computation.2 | async-start | bytes 8388608
  194.7 18.8 %slice-start.3 = ((s8[4718592]{0:T(1024)(128)(4,1)}), s8[524288]{0:T(1024)(128)(4,1)S(1)}, s32[]{:S(2)}) async-start(s8[4718592]{0:T(1024)(128)(4,1)} %bitcast.91), calls=%async_computation.3 | async-start | bytes 1048576
  203.6 9.8 %copy-start.9 = (f32[1024,768]{1,0:T(8,128)S(1)}, f32[1024,768]{1,0:T(8,128)}, u32[]{:S(2)}) copy-start(f32[1024,768]{1,0:T(8,128)} %copy-done.8) | copy-start | bytes 9437188
  228.6 2.5 copy-start.4
  284.0 8.8 %copy-start.5 = (f32[1024,768]{1,0:T(8,128)S(1)}, f32[1024,768]{1,0:T(8,128)}, u32[]{:S(2)}) copy-start(f32[1024,768]{1,0:T(8,128)} %copy-done.4) | copy-start | bytes 9437188
  284.0 8.8 %copy-start.7 = (bf16[1024,768]{1,0:T(8,128)(2,1)S(1)}, bf16[1024,768]{1,0:T(8,128)(2,1)}, u32[]{:S(2)}) copy-start(bf16[1024,768]{1,0:T(8,128)(2,1)} %get-tuple-element.64) | copy-start | bytes 4718596
  284.0 8.8 %copy-start.15 = (f32[1024]{0:T(1024)S(1)}, f32[1024]{0:T(1024)}, u32[]{:S(2)}) copy-start(f32[1024]{0:T(1024)} %copy-done.14) | copy-start | bytes 12292
  284.0 8.8 %copy-start.16 = (f32[768]{0:T(1024)S(1)}, f32[768]{0:T(1024)}, u32[]{:S(2)}) copy-start(f32[768]{0:T(1024)} %get-tuple-element.113) | copy-start | bytes 9220
  292.8 2.9 copy-start.19
  295.7 5.8 %copy-start.12 = (f32[6,2,8,256]{3,2,1,0:T(8,128)S(1)}, f32[6,2,8,256]{3,2,1,0:T(8,128)}, u32[]{:S(2)}) copy-start(f32[6,2,8,256]{3,2,1,0:T(8,128)} %get-tuple-element.74) | copy-start | bytes 294916
  295.7 5.8 %copy-start.10 = (f32[2048,32]{1,0:T(8,128)S(1)}, f32[2048,32]{1,0:T(8,128)}, u32[]{:S(2)}) copy-start(f32[2048,32]{1,0:T(8,128)} %constant.21.clone) | copy-start | bytes 786436
  (4 other events, 6.0 us)

commit v2 on v1

--- a/solution.py
+++ b/solution.py
@@ -206,13 +206,29 @@
 
 
 def loss_kernel(
-    n_dp, n_pair, x_ref, pos_ref, neg_ref, count_ref, loss_ref, grad_ref, by_dp, by_pair, unit, *sems
+    n_dp,
+    n_pair,
+    len_ref,
+    x_ref,
+    pos_ref,
+    neg_ref,
+    count_ref,
+    loss_ref,
+    grad_ref,
+    own,
+    by_dp,
+    by_pair,
+    unit,
+    *sems,
 ):
     rounds = Rounds(n_dp, n_pair, *sems)
+    docs, width = x_ref.shape
+    lengths = [len_ref[d].astype(jnp.float32) for d in range(docs)]
+    for d in range(docs):
+        own[d : d + 1] = x_ref[d : d + 1] / lengths[d]
     rounds.entered()
-    rounds.over_dp(x_ref, by_dp)
+    rounds.over_dp(own, by_dp)
     rounds.over_pair(by_dp, by_pair)
-    docs, width = x_ref.shape
     total = n_dp * n_pair * docs
     for d in range(n_dp):
         for p in range(n_pair):
@@ -258,21 +274,23 @@
 
             @pl.when((rounds.dp == d) & (rounds.pair == p))
             def _():
-                grad_ref[...] = unit[base : base + docs]
-
-
-def pooled_loss(pooled, positives, negatives, counts, cid):
+                for doc in range(docs):
+                    grad_ref[doc : doc + 1] = unit[base + doc : base + doc + 1] / lengths[doc]
+
+
+def pooled_loss(sums, lengths, positives, negatives, counts, cid):
     n_dp, n_pair = lax.axis_size("dp"), lax.axis_size("pair")
-    docs, width = pooled.shape
+    docs, width = sums.shape
     return pl.pallas_call(
         functools.partial(loss_kernel, n_dp, n_pair),
         out_shape=[
             jax.ShapeDtypeStruct((1, 1), jnp.float32),
-            jax.ShapeDtypeStruct(pooled.shape, jnp.float32),
+            jax.ShapeDtypeStruct(sums.shape, jnp.float32),
         ],
-        in_specs=[VM] * 4,
+        in_specs=[pl.BlockSpec(memory_space=pltpu.SMEM)] + [VM] * 4,
         out_specs=[VM] * 2,
         scratch_shapes=[
+            pltpu.VMEM((docs, width), jnp.float32),
             pltpu.VMEM((n_dp, docs, width), jnp.float32),
             pltpu.VMEM((n_pair, n_dp, docs, width), jnp.float32),
             pltpu.VMEM((n_dp * n_pair * docs, width), jnp.float32),
@@ -280,7 +298,7 @@
         + round_sems(n_dp, n_pair),
         compiler_params=pltpu.CompilerParams(collective_id=cid, has_side_effects=True),
         name="pooled_loss",
-    )(pooled, positives.reshape(1, -1), negatives.T, counts.reshape(1, -1))
+    )(lengths, sums, positives.reshape(1, -1), negatives.T, counts.reshape(1, -1))
 
 
 NT = (((1,), (1,)), ((), ()))
@@ -290,8 +308,12 @@
     tiles = seq // 128
     for d in range(1 - tiles, tiles):
         low = base + seq + 128 * d - 128
-        x = jnp.broadcast_to(w_ref[pl.ds(row, 1), low : low + 256], (128, 256))
-        tile = pltpu.roll(x, 0, 1, stride=1, stride_axis=0)[:, 128:]
+        line = w_ref[pl.ds(row, 1), low : low + 256]
+        if 128 * (abs(d) - 1) < REACH:
+            x = jnp.broadcast_to(line, (128, 256))
+            tile = pltpu.roll(x, 0, 1, stride=1, stride_axis=0)[:, 128:]
+        else:
+            tile = jnp.broadcast_to(line, (128, 256))[:, 128:]
         for a in range(tiles):
             if 0 <= a + d < tiles:
                 table[h, a * 128 : a * 128 + 128, (a + d) * 128 : (a + d) * 128 + 128] = tile
@@ -1685,18 +1707,14 @@
     output_rows = residual + jnp.dot(hidden, down_full, preferred_element_type=jnp.float32)
     normed_three, inverse_three = rms_forward(output_rows, norm_gains[2])
     live_rows = live.reshape(-1, 1)
-    length_float = lengths.astype(jnp.float32)
-    pooled_local = (
-        jnp.sum(
-            jnp.where(live_rows, normed_three, 0.0).reshape(doc_count, seq_len, model_width), axis=1
-        )
-        / length_float[:, None]
-    )
-    loss_cell, grad_pooled = pooled_loss(
-        pooled_local, positives, negatives, neg_counts, 3
+    live_sums = jnp.sum(
+        jnp.where(live_rows, normed_three, 0.0).reshape(doc_count, seq_len, model_width), axis=1
+    )
+    loss_cell, grad_sums = pooled_loss(
+        live_sums, lengths, positives, negatives, neg_counts, 3
     )
     grad_three = jnp.where(
-        live_rows, jnp.repeat(grad_pooled / length_float[:, None], seq_len, axis=0), 0.0
+        live_rows, jnp.repeat(grad_sums, seq_len, axis=0), 0.0
     )
     qkv_back, out_back, in_back, down_back = (qkv_full, out_full, in_full, down_full)
     grad_output, gain_three = rms_backward(output_rows, inverse_three, norm_gains[2], grad_three)

time: 478 us -> 473 us (0.990)
  no operation moved by 1% of the time
where the time goes in v2:
time: 473 us; the launch traced here: 464 us
  Pallas kernels  367 us (78%)
  matrix products  75 us (16%)
  other arithmetic  12 us (3%)
  local copies, waits for them, and re-layouts  8.33 us (2%)
    pallas_call x1, Pallas kernels, back(): pl.pallas_call(functools.partial(back_kernel, n_dp, n_pair, pieces, len(g...  134 us
    pallas_call x1, Pallas kernels, front(): pl.pallas_call(functools.partial(front_kernel, n_dp, n_pair, pieces, len(...  118 us
    pallas_call x1, Pallas kernels, attention_back(): pl.pallas_call(functools.partial(backward_kernel, n_dp, n_pair, pieces, l...  48.8 us
    pallas_call x1, Pallas kernels, update(): pl.pallas_call(functools.partial(update_kernel, len(grads)), grid=(steps,...  31.8 us
    pallas_call x1, Pallas kernels, attention(): pl.pallas_call(forward_kernel, grid_spec=pltpu.PrefetchScalarGridSpec(num...  20.1 us
    pallas_call x1, Pallas kernels, pooled_loss(): pl.pallas_call(functools.partial(loss_kernel, n_dp, n_pair), out_shape=[j...  14.8 us
    dot_general x1, matrix products, local_fast(): lax.dot_general(hidden, grad_branch, CONTRACT_ROWS, preferred_element_typ...  9.82 us

profile of v2, /device:TPU:0, one launch (start us, length us, event | category | flops | bytes accessed | tf_op | source)
XLA Modules:
  0.0 464.3 jit_solution(11018548053171333242)
XLA Ops:
  4.7 1.9 convolution_bitcast_fusion.w_ref.refs_5_
  6.6 118.1 %rows_and_weights.1 = (bf16[1024,768]{1,0:T(8,128)(2,1)}, s32[1,1024]{1,0:T(1,128)}, s32[8,1,256]{2,1,0:T(1,128)}, bf16[32,24,2304]{2,1,0:T(8,128)(2,1)}, bf16[3...) custom-call(s32[2,512]{1,0:T(2,128)} %bitcast.81, s32[2,512]{1,0:T(2,128)} %refs_1_.1, ...), custom_call_target="tpu_custom_call" | custom-call | tf_op jit(solution)/shard_map/rows_and_weights/pallas_call | solution.py:661
  124.7 1.8 fusion.11
  127.1 8.8 %convolution_convert_fusion.q_ref.k_ref.v_ref.refs_1_.refs_2_.refs_3_ = bf16[1024,2304]{1,0:T(8,128)(2,1)} fusion(bf16[768,2304]{1,0:T(8,128)(2,1)} %bitcast.98, bf16[1024,768]{1,0:T(8,128)(2,1)} %get-tuple-element.64, f32[768]{0:T(1024)} %get-tuple-element.113, f32[1024]{0:T(1024)S(1)} %add_rsqrt_fusion.2), kind=kOutput, calls=%fused_computation.2 | convolution fusion | flops 3629383680 | bytes 9837568 | tf_op jit(solution)/shard_map/dot_general | solution.py:1697
  135.9 20.1 %attention.1 = bf16[1024,768]{1,0:T(8,128)(2,1)S(1)} custom-call(s32[2]{0:T(128)S(1)} %copy-done.1, bf16[1024,2304]{1,0:T(8,128)(2,1)} %convolution_convert_fusion.q_ref.k_ref.v_ref.refs_1_.refs_2_.refs_3_, bf16[1024,2304]{1,0:T(8,128)(2,1)} %convolution_convert_fusion.q_ref.k_ref.v_ref.refs_1_.refs_2_.refs_3_, ...), custom_call_target="tpu_custom_call" | custom-call | tf_op jit(solution)/shard_map/attention/pallas_call | solution.py:349
  156.0 1.5 multiply_reduce_fusion.3
  157.6 5.8 %maximum_convert_fusion = bf16[1024,3072]{1,0:T(8,128)(2,1)S(1)} fusion(bf16[768,3072]{1,0:T(8,128)(2,1)S(1)} %bitcast.90, f32[1024,768]{1,0:T(8,128)S(1)} %get-tuple-element.115, f32[768]{0:T(1024)S(1)} %copy-done.18, f32[1024]{0:T(1024)S(1)} %add_rsqrt_fusion.1), kind=kOutput, calls=%fused_computation.1 | convolution fusion | flops 4840488960 | bytes 14162944 | tf_op jit(solution)/shard_map/dot_general | solution.py:1704
  163.5 5.3 %multiply_reduce_fusion.2 = (f32[1024]{0:T(1024)S(1)}, f32[1024,768]{1,0:T(8,128)S(1)}) fusion(f32[1024,768]{1,0:T(8,128)S(1)} %get-tuple-element.115, bf16[1024,3072]{1,0:T(8,128)(2,1)S(1)} %maximum_convert_fusion, bf16[3072,768]{1,0:T(8,128)(2,1)S(1)} %bitcast.97), kind=kOutput, calls=%fused_computation.34 | convolution fusion | flops 4834196480 | bytes 17305600 | tf_op jit(solution)/shard_map/dot_general | solution.py:1707
  168.8 1.6 copy-done.2
  171.6 14.8 %pooled_loss.1 = (f32[1,1]{1,0:T(1,128)}, f32[2,768]{1,0:T(2,128)}) custom-call(s32[2]{0:T(128)} %refs_0_.1, f32[2,768]{1,0:T(2,128)} %bitcast_reduce_fusion.x_ref, s32[1,64]{1,0:T(1,128)} %bitcast.86, s32[7,64]{1,0:T(8,128)} %bitcast.85, s32[1,64]{1,0:T(1,128)} %bitcast.87), custom_call_target="tpu_custom_call" | custom-call | tf_op jit(solution)/shard_map/pooled_loss/pallas_call | solution.py:284
  186.4 3.4 fusion.18
  191.5 8.9 %select_convert_fusion = bf16[1024,3072]{1,0:T(8,128)(2,1)S(1)} fusion(bf16[1024,3072]{1,0:T(8,128)(2,1)} %copy-done.21, bf16[1024,768]{1,0:T(8,128)(2,1)S(1)} %fusion.19, bf16[3072,768]{1,0:T(8,128)(2,1)} %bitcast.94), kind=kOutput, calls=%fused_computation | convolution fusion | flops 4841275392 | bytes 18874368 | tf_op jit(solution)/shard_map/dot_general | solution.py:1725
  200.4 9.8 %convolution_convert_fusion.2 = bf16[3072,768]{1,0:T(8,128)(2,1)} fusion(bf16[1024,3072]{1,0:T(8,128)(2,1)} %copy-done.21, bf16[1024,768]{1,0:T(8,128)(2,1)S(1)} %fusion.19), kind=kOutput, calls=%fused_computation.4 | convolution fusion | flops 4834197504 | bytes 12582912 | tf_op jit(solution)/shard_map/dot_general | solution.py:1722
  210.2 5.5 %multiply_reduce_fusion = (f32[768]{0:T(1024)S(1)}, f32[1024]{0:T(1024)S(1)}, f32[1024,768]{1,0:T(8,128)S(1)}) fusion(f32[1024,768]{1,0:T(8,128)S(1)} %copy-done.9, f32[1024]{0:T(1024)S(1)} %add_rsqrt_fusion.1, f32[768]{0:T(1024)S(1)} %copy-done.18, bf16[1024,3072]{1,0:T(8,128)(2,1)S(1)} %select_convert_fusion, bf16[768,3072]{1,0:T(8,128)(2,1)S(1)} %bitcast.93), kind=kOutput, calls=%fused_computation.30 | convolution fusion | flops 4836554752 | bytes 17315840 | tf_op jit(solution)/shard_map/dot_general | solution.py:1732
  215.7 7.2 %convolution_convert_fusion.1 = bf16[768,3072]{1,0:T(8,128)(2,1)} fusion(bf16[1024,3072]{1,0:T(8,128)(2,1)S(1)} %select_convert_fusion, f32[1024,768]{1,0:T(8,128)S(1)} %copy-done.9, f32[768]{0:T(1024)S(1)} %copy-done.18, f32[1024]{0:T(1024)S(1)} %add_rsqrt_fusion.1), kind=kOutput, calls=%fused_computation.3 | convolution fusion | flops 4836556800 | bytes 14162944 | tf_op jit(solution)/shard_map/dot_general | solution.py:1729
  223.5 1.8 multiply_add_fusion
  225.3 2.5 convolution_convert_fusion.5
  227.9 2.7 convolution_convert_fusion.4.refs_4_
  230.5 48.8 %attention_back.1 = (bf16[1024,2304]{1,0:T(8,128)(2,1)}, f32[6,2,8,256]{3,2,1,0:T(8,128)}, f32[1,1]{1,0:T(1,128)}, f32[96,768]{1,0:T(8,128)}) custom-call(s32[2]{0:T(128)} %refs_0_.1, bf16[1024,2304]{1,0:T(8,128)(2,1)} %convolution_convert_fusion.q_ref.k_ref.v_ref.refs_1_.refs_2_.refs_3_, ...), custom_call_target="tpu_custom_call" | custom-call | tf_op jit(solution)/shard_map/attention_back/pallas_call | solution.py:948
  279.4 8.2 %fusion.10 = (f32[768]{0:T(1024)S(1)}, f32[1024]{0:T(1024)S(1)}, f32[1024,768]{1,0:T(8,128)S(1)}) fusion(bf16[1024,768]{1,0:T(8,128)(2,1)} %get-tuple-element.64, f32[1024]{0:T(1024)} %copy-done.15, f32[768]{0:T(1024)} %get-tuple-element.113, bf16[1024,2304]{1,0:T(8,128)(2,1)} %get-tuple-element.70, bf16[768,2304]{1,0:T(8,128)(2,1)} %bitcast.99), kind=kOutput, calls=%fused_computation.19 | convolution fusion | flops 3629381888 | bytes 12990464 | tf_op jit(solution)/shard_map/dot_general | solution.py:1763
  288.2 2.0 fusion.9.refs_0_
  291.1 5.8 %convolution_convert_fusion.3 = bf16[768,2304]{1,0:T(8,128)(2,1)} fusion(bf16[1024,2304]{1,0:T(8,128)(2,1)S(1)} %copy-done.19, bf16[1024,768]{1,0:T(8,128)(2,1)S(1)} %copy-done.7, f32[768]{0:T(1024)S(1)} %copy-done.17, f32[1024]{0:T(1024)S(1)} %copy-done.16), kind=kOutput, calls=%fused_computation.5 | convolution fusion | flops 3628793856 | bytes 9837568 | tf_op jit(solution)/shard_map/dot_general | solution.py:1760
  298.1 133.9 %table_and_weights.1 = (bf16[4096,768]{1,0:T(8,128)(2,1)}, f32[40,128]{1,0:T(8,128)}, f32[24,2304]{1,0:T(8,128)}, f32[24,768]{1,0:T(8,128)}, f32[24,3072]{1,0:T(8,128)}) custom-call(bf16[1024,768]{1,0:T(8,128)(2,1)} %fusion.9.refs_0_, s32[1,1024]{1,0:T(1,128)} %get-tuple-element.71.refs_1_, s32[1,2048]{1,0:T(1,128)} %bitcast.84, ...), custom_call_target="tpu_custom_call" | custom-call | tf_op jit(solution)/shard_map/table_and_weights/pallas_call | solution.py:1242
  432.0 31.8 %update.1 = (f32[1,1]{1,0:T(1,128)}, f32[1,1]{1,0:T(1,128)}, f32[4016,768]{1,0:T(8,128)}, f32[4016,768]{1,0:T(8,128)}, f32[4016,768]{1,0:T(8,128)}, /*index=5*/f...) custom-call(f32[40,128]{1,0:T(8,128)} %get-tuple-element.75.refs_0_,, ...), custom_call_target="tpu_custom_call" | custom-call | tf_op jit(solution)/shard_map/update/pallas_call | solution.py:1360
  (76 shorter events, 10.8 us)
Async XLA Ops:
  127.1 8.8 %copy-start = (f32[12,2048]{1,0:T(8,128)S(1)}, f32[12,2048]{1,0:T(8,128)}, u32[]{:S(2)}) copy-start(f32[12,2048]{1,0:T(8,128)} %convolution_bitcast_fusion.w_ref.refs_5_) | copy-start | bytes 294916
  127.1 8.8 %copy-start.1 = (s32[2]{0:T(128)S(1)}, s32[2]{0:T(128)}, u32[]{:S(2)}) copy-start(s32[2]{0:T(128)} %refs_0_.1) | copy-start | bytes 28
  127.1 30.5 %slice-start = ((s8[4718592]{0:T(1024)(128)(4,1)}), s8[4194304]{0:T(1024)(128)(4,1)S(1)}, s32[]{:S(2)}) async-start(s8[4718592]{0:T(1024)(128)(4,1)} %bitcast.88), calls=%async_computation | async-start | bytes 8388608
  135.9 20.1 %copy-start.6 = (bf16[1024,768]{1,0:T(8,128)(2,1)S(1)}, bf16[1024,768]{1,0:T(8,128)(2,1)}, u32[]{:S(2)}) copy-start(bf16[1024,768]{1,0:T(8,128)(2,1)} %get-tuple-element.64) | copy-start | bytes 4718596
  135.9 20.1 %copy-start.20 = (bf16[32,24,768]{2,1,0:T(8,128)(2,1)S(1)}, bf16[32,24,768]{2,1,0:T(8,128)(2,1)}, u32[]{:S(2)}) copy-start(bf16[32,24,768]{2,1,0:T(8,128)(2,1)} %get-tuple-element.66) | copy-start | bytes 3538948
  135.9 21.7 %slice-start.1 = ((s8[4718592]{0:T(1024)(128)(4,1)}), s8[524288]{0:T(1024)(128)(4,1)S(1)}, s32[]{:S(2)}) async-start(s8[4718592]{0:T(1024)(128)(4,1)} %bitcast.88), calls=%async_computation.1 | async-start | bytes 1048576
  156.0 7.5 %slice-start.4 = ((s8[4718592]{0:T(1024)(128)(4,1)}), s8[4194304]{0:T(1024)(128)(4,1)S(1)}, s32[]{:S(2)}) async-start(s8[4718592]{0:T(1024)(128)(4,1)} %bitcast.95), calls=%async_computation.4 | async-start | bytes 8388608
  157.5 5.9 %copy-start.8 = (f32[1024,768]{1,0:T(8,128)}, f32[1024,768]{1,0:T(8,128)S(1)}, u32[]{:S(2)}) copy-start(f32[1024,768]{1,0:T(8,128)S(1)} %get-tuple-element.115) | copy-start | bytes 9437188
  157.6 5.9 %slice-start.5 = ((s8[4718592]{0:T(1024)(128)(4,1)}), s8[524288]{0:T(1024)(128)(4,1)S(1)}, s32[]{:S(2)}) async-start(s8[4718592]{0:T(1024)(128)(4,1)} %bitcast.95), calls=%async_computation.5 | async-start | bytes 1048576
  163.5 5.3 %copy-start.21 = (bf16[1024,3072]{1,0:T(8,128)(2,1)}, bf16[1024,3072]{1,0:T(8,128)(2,1)S(1)}, u32[]{:S(2)}) copy-start(bf16[1024,3072]{1,0:T(8,128)(2,1)S(1)} %maximum_convert_fusion) | copy-start | bytes 18874372
  163.5 7.0 %copy-start.11 = (f32[768]{0:T(1024)S(1)}, f32[768]{0:T(1024)}, u32[]{:S(2)}) copy-start(f32[768]{0:T(1024)} %get-tuple-element.111) | copy-start | bytes 9220
  163.5 7.0 %copy-start.14 = (pred[1024]{0:T(1024)(128)(4,1)S(1)}, pred[1024]{0:T(1024)(128)(4,1)}, u32[]{:S(2)}) copy-start(pred[1024]{0:T(1024)(128)(4,1)} %lt.23) | copy-start | bytes 3076
  186.4 4.0 copy-start.3
  186.4 4.0 copy-start.13
  190.4 19.8 %slice-start.2 = ((s8[4718592]{0:T(1024)(128)(4,1)}), s8[4194304]{0:T(1024)(128)(4,1)S(1)}, s32[]{:S(2)}) async-start(s8[4718592]{0:T(1024)(128)(4,1)} %bitcast.91), calls=%async_computation.2 | async-start | bytes 8388608
  191.5 18.7 %slice-start.3 = ((s8[4718592]{0:T(1024)(128)(4,1)}), s8[524288]{0:T(1024)(128)(4,1)S(1)}, s32[]{:S(2)}) async-start(s8[4718592]{0:T(1024)(128)(4,1)} %bitcast.91), calls=%async_computation.3 | async-start | bytes 1048576
  200.4 9.8 %copy-start.9 = (f32[1024,768]{1,0:T(8,128)S(1)}, f32[1024,768]{1,0:T(8,128)}, u32[]{:S(2)}) copy-start(f32[1024,768]{1,0:T(8,128)} %copy-done.8) | copy-start | bytes 9437188
  279.4 8.8 %copy-start.5 = (f32[1024,768]{1,0:T(8,128)S(1)}, f32[1024,768]{1,0:T(8,128)}, u32[]{:S(2)}) copy-start(f32[1024,768]{1,0:T(8,128)} %copy-done.4) | copy-start | bytes 9437188
  279.4 8.8 %copy-start.7 = (bf16[1024,768]{1,0:T(8,128)(2,1)S(1)}, bf16[1024,768]{1,0:T(8,128)(2,1)}, u32[]{:S(2)}) copy-start(bf16[1024,768]{1,0:T(8,128)(2,1)} %get-tuple-element.64) | copy-start | bytes 4718596
  279.4 8.8 %copy-start.16 = (f32[1024]{0:T(1024)S(1)}, f32[1024]{0:T(1024)}, u32[]{:S(2)}) copy-start(f32[1024]{0:T(1024)} %copy-done.15) | copy-start | bytes 12292
  279.4 8.8 %copy-start.17 = (f32[768]{0:T(1024)S(1)}, f32[768]{0:T(1024)}, u32[]{:S(2)}) copy-start(f32[768]{0:T(1024)} %get-tuple-element.113) | copy-start | bytes 9220
  288.2 2.9 copy-start.19
  291.1 5.8 %copy-start.12 = (f32[6,2,8,256]{3,2,1,0:T(8,128)S(1)}, f32[6,2,8,256]{3,2,1,0:T(8,128)}, u32[]{:S(2)}) copy-start(f32[6,2,8,256]{3,2,1,0:T(8,128)} %get-tuple-element.74) | copy-start | bytes 294916
  291.1 5.8 %copy-start.10 = (f32[2048,32]{1,0:T(8,128)S(1)}, f32[2048,32]{1,0:T(8,128)}, u32[]{:S(2)}) copy-start(f32[2048,32]{1,0:T(8,128)} %constant.21.clone) | copy-start | bytes 786436
  (4 other events, 6.4 us)

commit v3 on v2

--- a/solution.py
+++ b/solution.py
@@ -387,9 +387,11 @@
 
 
 def weight_pieces(widths):
+    first = widths[0] * 2 // 3 // 128 * 128
     cut = widths[3] * 2 // 3 // 128 * 128
     return [
-        (0, 0, widths[0], 1),
+        (0, 0, first, 0),
+        (0, first, widths[0], 1),
         (2, 0, widths[2], 0),
         (1, 0, widths[1], 0),
         (3, 0, cut, 0),

time: 473 us -> 470 us (level)
  no operation moved by 1% of the time
where the time goes in v3:
time: 470 us; the launch traced here: 461 us
  Pallas kernels  364 us (77%)
  matrix products  75 us (16%)
  other arithmetic  12 us (3%)
  local copies, waits for them, and re-layouts  8.33 us (2%)
    pallas_call x1, Pallas kernels, back(): pl.pallas_call(functools.partial(back_kernel, n_dp, n_pair, pieces, len(g...  134 us
    pallas_call x1, Pallas kernels, front(): pl.pallas_call(functools.partial(front_kernel, n_dp, n_pair, pieces, len(...  114 us
    pallas_call x1, Pallas kernels, attention_back(): pl.pallas_call(functools.partial(backward_kernel, n_dp, n_pair, pieces, l...  48.8 us
    pallas_call x1, Pallas kernels, update(): pl.pallas_call(functools.partial(update_kernel, len(grads)), grid=(steps,...  31.8 us
    pallas_call x1, Pallas kernels, attention(): pl.pallas_call(forward_kernel, grid_spec=pltpu.PrefetchScalarGridSpec(num...  20.1 us
    pallas_call x1, Pallas kernels, pooled_loss(): pl.pallas_call(functools.partial(loss_kernel, n_dp, n_pair), out_shape=[j...  14.8 us
    dot_general x1, matrix products, local_fast(): lax.dot_general(hidden, grad_branch, CONTRACT_ROWS, preferred_element_typ...  9.82 us

profile of v3, /device:TPU:0, one launch (start us, length us, event | category | flops | bytes accessed | tf_op | source)
XLA Modules:
  0.0 460.6 jit_solution(17484973859089503759)
XLA Ops:
  4.7 1.9 convolution_bitcast_fusion.w_ref.refs_5_
  6.6 114.4 %rows_and_weights.1 = (bf16[1024,768]{1,0:T(8,128)(2,1)}, s32[1,1024]{1,0:T(1,128)}, s32[8,1,256]{2,1,0:T(1,128)}, bf16[32,24,2304]{2,1,0:T(8,128)(2,1)}, bf16[3...) custom-call(s32[2,512]{1,0:T(2,128)} %bitcast.81, s32[2,512]{1,0:T(2,128)} %refs_1_.1, ...), custom_call_target="tpu_custom_call" | custom-call | tf_op jit(solution)/shard_map/rows_and_weights/pallas_call | solution.py:663
  121.0 1.8 fusion.11
  123.4 8.8 %convolution_convert_fusion.q_ref.k_ref.v_ref.refs_1_.refs_2_.refs_3_ = bf16[1024,2304]{1,0:T(8,128)(2,1)} fusion(bf16[768,2304]{1,0:T(8,128)(2,1)} %bitcast.98, bf16[1024,768]{1,0:T(8,128)(2,1)} %get-tuple-element.64, f32[768]{0:T(1024)} %get-tuple-element.113, f32[1024]{0:T(1024)S(1)} %add_rsqrt_fusion.2), kind=kOutput, calls=%fused_computation.2 | convolution fusion | flops 3629383680 | bytes 9837568 | tf_op jit(solution)/shard_map/dot_general | solution.py:1699
  132.2 20.1 %attention.1 = bf16[1024,768]{1,0:T(8,128)(2,1)S(1)} custom-call(s32[2]{0:T(128)S(1)} %copy-done.1, bf16[1024,2304]{1,0:T(8,128)(2,1)} %convolution_convert_fusion.q_ref.k_ref.v_ref.refs_1_.refs_2_.refs_3_, bf16[1024,2304]{1,0:T(8,128)(2,1)} %convolution_convert_fusion.q_ref.k_ref.v_ref.refs_1_.refs_2_.refs_3_, ...), custom_call_target="tpu_custom_call" | custom-call | tf_op jit(solution)/shard_map/attention/pallas_call | solution.py:349
  152.3 1.5 multiply_reduce_fusion.3
  153.9 5.8 %maximum_convert_fusion = bf16[1024,3072]{1,0:T(8,128)(2,1)S(1)} fusion(bf16[768,3072]{1,0:T(8,128)(2,1)S(1)} %bitcast.90, f32[1024,768]{1,0:T(8,128)S(1)} %get-tuple-element.115, f32[768]{0:T(1024)S(1)} %copy-done.18, f32[1024]{0:T(1024)S(1)} %add_rsqrt_fusion.1), kind=kOutput, calls=%fused_computation.1 | convolution fusion | flops 4840488960 | bytes 14162944 | tf_op jit(solution)/shard_map/dot_general | solution.py:1706
  159.8 5.3 %multiply_reduce_fusion.2 = (f32[1024]{0:T(1024)S(1)}, f32[1024,768]{1,0:T(8,128)S(1)}) fusion(f32[1024,768]{1,0:T(8,128)S(1)} %get-tuple-element.115, bf16[1024,3072]{1,0:T(8,128)(2,1)S(1)} %maximum_convert_fusion, bf16[3072,768]{1,0:T(8,128)(2,1)S(1)} %bitcast.97), kind=kOutput, calls=%fused_computation.34 | convolution fusion | flops 4834196480 | bytes 17305600 | tf_op jit(solution)/shard_map/dot_general | solution.py:1709
  165.1 1.6 copy-done.2
  167.9 14.8 %pooled_loss.1 = (f32[1,1]{1,0:T(1,128)}, f32[2,768]{1,0:T(2,128)}) custom-call(s32[2]{0:T(128)} %refs_0_.1, f32[2,768]{1,0:T(2,128)} %bitcast_reduce_fusion.x_ref, s32[1,64]{1,0:T(1,128)} %bitcast.86, s32[7,64]{1,0:T(8,128)} %bitcast.85, s32[1,64]{1,0:T(1,128)} %bitcast.87), custom_call_target="tpu_custom_call" | custom-call | tf_op jit(solution)/shard_map/pooled_loss/pallas_call | solution.py:284
  182.7 3.4 fusion.18
  187.8 8.9 %select_convert_fusion = bf16[1024,3072]{1,0:T(8,128)(2,1)S(1)} fusion(bf16[1024,3072]{1,0:T(8,128)(2,1)} %copy-done.21, bf16[1024,768]{1,0:T(8,128)(2,1)S(1)} %fusion.19, bf16[3072,768]{1,0:T(8,128)(2,1)} %bitcast.94), kind=kOutput, calls=%fused_computation | convolution fusion | flops 4841275392 | bytes 18874368 | tf_op jit(solution)/shard_map/dot_general | solution.py:1727
  196.6 9.8 %convolution_convert_fusion.2 = bf16[3072,768]{1,0:T(8,128)(2,1)} fusion(bf16[1024,3072]{1,0:T(8,128)(2,1)} %copy-done.21, bf16[1024,768]{1,0:T(8,128)(2,1)S(1)} %fusion.19), kind=kOutput, calls=%fused_computation.4 | convolution fusion | flops 4834197504 | bytes 12582912 | tf_op jit(solution)/shard_map/dot_general | solution.py:1724
  206.5 5.5 %multiply_reduce_fusion = (f32[768]{0:T(1024)S(1)}, f32[1024]{0:T(1024)S(1)}, f32[1024,768]{1,0:T(8,128)S(1)}) fusion(f32[1024,768]{1,0:T(8,128)S(1)} %copy-done.9, f32[1024]{0:T(1024)S(1)} %add_rsqrt_fusion.1, f32[768]{0:T(1024)S(1)} %copy-done.18, bf16[1024,3072]{1,0:T(8,128)(2,1)S(1)} %select_convert_fusion, bf16[768,3072]{1,0:T(8,128)(2,1)S(1)} %bitcast.93), kind=kOutput, calls=%fused_computation.30 | convolution fusion | flops 4836554752 | bytes 17315840 | tf_op jit(solution)/shard_map/dot_general | solution.py:1734
  212.0 7.2 %convolution_convert_fusion.1 = bf16[768,3072]{1,0:T(8,128)(2,1)} fusion(bf16[1024,3072]{1,0:T(8,128)(2,1)S(1)} %select_convert_fusion, f32[1024,768]{1,0:T(8,128)S(1)} %copy-done.9, f32[768]{0:T(1024)S(1)} %copy-done.18, f32[1024]{0:T(1024)S(1)} %add_rsqrt_fusion.1), kind=kOutput, calls=%fused_computation.3 | convolution fusion | flops 4836556800 | bytes 14162944 | tf_op jit(solution)/shard_map/dot_general | solution.py:1731
  219.8 1.8 multiply_add_fusion
  221.6 2.5 convolution_convert_fusion.5
  224.1 2.7 convolution_convert_fusion.4.refs_4_
  226.8 48.8 %attention_back.1 = (bf16[1024,2304]{1,0:T(8,128)(2,1)}, f32[6,2,8,256]{3,2,1,0:T(8,128)}, f32[1,1]{1,0:T(1,128)}, f32[96,768]{1,0:T(8,128)}) custom-call(s32[2]{0:T(128)} %refs_0_.1, bf16[1024,2304]{1,0:T(8,128)(2,1)} %convolution_convert_fusion.q_ref.k_ref.v_ref.refs_1_.refs_2_.refs_3_, ...), custom_call_target="tpu_custom_call" | custom-call | tf_op jit(solution)/shard_map/attention_back/pallas_call | solution.py:950
  275.7 8.2 %fusion.10 = (f32[768]{0:T(1024)S(1)}, f32[1024]{0:T(1024)S(1)}, f32[1024,768]{1,0:T(8,128)S(1)}) fusion(bf16[1024,768]{1,0:T(8,128)(2,1)} %get-tuple-element.64, f32[1024]{0:T(1024)} %copy-done.15, f32[768]{0:T(1024)} %get-tuple-element.113, bf16[1024,2304]{1,0:T(8,128)(2,1)} %get-tuple-element.70, bf16[768,2304]{1,0:T(8,128)(2,1)} %bitcast.99), kind=kOutput, calls=%fused_computation.19 | convolution fusion | flops 3629381888 | bytes 12990464 | tf_op jit(solution)/shard_map/dot_general | solution.py:1765
  284.5 2.0 fusion.9.refs_0_
  287.4 5.8 %convolution_convert_fusion.3 = bf16[768,2304]{1,0:T(8,128)(2,1)} fusion(bf16[1024,2304]{1,0:T(8,128)(2,1)S(1)} %copy-done.19, bf16[1024,768]{1,0:T(8,128)(2,1)S(1)} %copy-done.7, f32[768]{0:T(1024)S(1)} %copy-done.17, f32[1024]{0:T(1024)S(1)} %copy-done.16), kind=kOutput, calls=%fused_computation.5 | convolution fusion | flops 3628793856 | bytes 9837568 | tf_op jit(solution)/shard_map/dot_general | solution.py:1762
  294.4 133.9 %table_and_weights.1 = (bf16[4096,768]{1,0:T(8,128)(2,1)}, f32[40,128]{1,0:T(8,128)}, f32[24,2304]{1,0:T(8,128)}, f32[24,768]{1,0:T(8,128)}, f32[24,3072]{1,0:T(8,128)}) custom-call(bf16[1024,768]{1,0:T(8,128)(2,1)} %fusion.9.refs_0_, s32[1,1024]{1,0:T(1,128)} %get-tuple-element.71.refs_1_, s32[1,2048]{1,0:T(1,128)} %bitcast.84, ...), custom_call_target="tpu_custom_call" | custom-call | tf_op jit(solution)/shard_map/table_and_weights/pallas_call | solution.py:1244
  428.3 31.8 %update.1 = (f32[1,1]{1,0:T(1,128)}, f32[1,1]{1,0:T(1,128)}, f32[4016,768]{1,0:T(8,128)}, f32[4016,768]{1,0:T(8,128)}, f32[4016,768]{1,0:T(8,128)}, /*index=5*/f...) custom-call(f32[40,128]{1,0:T(8,128)} %get-tuple-element.75.refs_0_,, ...), custom_call_target="tpu_custom_call" | custom-call | tf_op jit(solution)/shard_map/update/pallas_call | solution.py:1362
  (76 shorter events, 10.8 us)
Async XLA Ops:
  123.4 8.8 %copy-start = (f32[12,2048]{1,0:T(8,128)S(1)}, f32[12,2048]{1,0:T(8,128)}, u32[]{:S(2)}) copy-start(f32[12,2048]{1,0:T(8,128)} %convolution_bitcast_fusion.w_ref.refs_5_) | copy-start | bytes 294916
  123.4 8.8 %copy-start.1 = (s32[2]{0:T(128)S(1)}, s32[2]{0:T(128)}, u32[]{:S(2)}) copy-start(s32[2]{0:T(128)} %refs_0_.1) | copy-start | bytes 28
  123.4 30.5 %slice-start = ((s8[4718592]{0:T(1024)(128)(4,1)}), s8[4194304]{0:T(1024)(128)(4,1)S(1)}, s32[]{:S(2)}) async-start(s8[4718592]{0:T(1024)(128)(4,1)} %bitcast.88), calls=%async_computation | async-start | bytes 8388608
  132.2 20.1 %copy-start.6 = (bf16[1024,768]{1,0:T(8,128)(2,1)S(1)}, bf16[1024,768]{1,0:T(8,128)(2,1)}, u32[]{:S(2)}) copy-start(bf16[1024,768]{1,0:T(8,128)(2,1)} %get-tuple-element.64) | copy-start | bytes 4718596
  132.2 20.1 %copy-start.20 = (bf16[32,24,768]{2,1,0:T(8,128)(2,1)S(1)}, bf16[32,24,768]{2,1,0:T(8,128)(2,1)}, u32[]{:S(2)}) copy-start(bf16[32,24,768]{2,1,0:T(8,128)(2,1)} %get-tuple-element.66) | copy-start | bytes 3538948
  132.2 21.7 %slice-start.1 = ((s8[4718592]{0:T(1024)(128)(4,1)}), s8[524288]{0:T(1024)(128)(4,1)S(1)}, s32[]{:S(2)}) async-start(s8[4718592]{0:T(1024)(128)(4,1)} %bitcast.88), calls=%async_computation.1 | async-start | bytes 1048576
  152.3 7.5 %slice-start.4 = ((s8[4718592]{0:T(1024)(128)(4,1)}), s8[4194304]{0:T(1024)(128)(4,1)S(1)}, s32[]{:S(2)}) async-start(s8[4718592]{0:T(1024)(128)(4,1)} %bitcast.95), calls=%async_computation.4 | async-start | bytes 8388608
  153.8 5.9 %copy-start.8 = (f32[1024,768]{1,0:T(8,128)}, f32[1024,768]{1,0:T(8,128)S(1)}, u32[]{:S(2)}) copy-start(f32[1024,768]{1,0:T(8,128)S(1)} %get-tuple-element.115) | copy-start | bytes 9437188
  153.9 5.9 %slice-start.5 = ((s8[4718592]{0:T(1024)(128)(4,1)}), s8[524288]{0:T(1024)(128)(4,1)S(1)}, s32[]{:S(2)}) async-start(s8[4718592]{0:T(1024)(128)(4,1)} %bitcast.95), calls=%async_computation.5 | async-start | bytes 1048576
  159.8 5.3 %copy-start.21 = (bf16[1024,3072]{1,0:T(8,128)(2,1)}, bf16[1024,3072]{1,0:T(8,128)(2,1)S(1)}, u32[]{:S(2)}) copy-start(bf16[1024,3072]{1,0:T(8,128)(2,1)S(1)} %maximum_convert_fusion) | copy-start | bytes 18874372
  159.8 7.0 %copy-start.11 = (f32[768]{0:T(1024)S(1)}, f32[768]{0:T(1024)}, u32[]{:S(2)}) copy-start(f32[768]{0:T(1024)} %get-tuple-element.111) | copy-start | bytes 9220
  159.8 7.0 %copy-start.14 = (pred[1024]{0:T(1024)(128)(4,1)S(1)}, pred[1024]{0:T(1024)(128)(4,1)}, u32[]{:S(2)}) copy-start(pred[1024]{0:T(1024)(128)(4,1)} %lt.23) | copy-start | bytes 3076
  182.7 4.0 copy-start.3
  182.7 4.0 copy-start.13
  186.7 19.8 %slice-start.2 = ((s8[4718592]{0:T(1024)(128)(4,1)}), s8[4194304]{0:T(1024)(128)(4,1)S(1)}, s32[]{:S(2)}) async-start(s8[4718592]{0:T(1024)(128)(4,1)} %bitcast.91), calls=%async_computation.2 | async-start | bytes 8388608
  187.7 18.7 %slice-start.3 = ((s8[4718592]{0:T(1024)(128)(4,1)}), s8[524288]{0:T(1024)(128)(4,1)S(1)}, s32[]{:S(2)}) async-start(s8[4718592]{0:T(1024)(128)(4,1)} %bitcast.91), calls=%async_computation.3 | async-start | bytes 1048576
  196.6 9.8 %copy-start.9 = (f32[1024,768]{1,0:T(8,128)S(1)}, f32[1024,768]{1,0:T(8,128)}, u32[]{:S(2)}) copy-start(f32[1024,768]{1,0:T(8,128)} %copy-done.8) | copy-start | bytes 9437188
  275.6 8.8 %copy-start.5 = (f32[1024,768]{1,0:T(8,128)S(1)}, f32[1024,768]{1,0:T(8,128)}, u32[]{:S(2)}) copy-start(f32[1024,768]{1,0:T(8,128)} %copy-done.4) | copy-start | bytes 9437188
  275.6 8.8 %copy-start.7 = (bf16[1024,768]{1,0:T(8,128)(2,1)S(1)}, bf16[1024,768]{1,0:T(8,128)(2,1)}, u32[]{:S(2)}) copy-start(bf16[1024,768]{1,0:T(8,128)(2,1)} %get-tuple-element.64) | copy-start | bytes 4718596
  275.7 8.8 %copy-start.16 = (f32[1024]{0:T(1024)S(1)}, f32[1024]{0:T(1024)}, u32[]{:S(2)}) copy-start(f32[1024]{0:T(1024)} %copy-done.15) | copy-start | bytes 12292
  275.7 8.8 %copy-start.17 = (f32[768]{0:T(1024)S(1)}, f32[768]{0:T(1024)}, u32[]{:S(2)}) copy-start(f32[768]{0:T(1024)} %get-tuple-element.113) | copy-start | bytes 9220
  284.4 2.9 copy-start.19
  287.4 5.8 %copy-start.12 = (f32[6,2,8,256]{3,2,1,0:T(8,128)S(1)}, f32[6,2,8,256]{3,2,1,0:T(8,128)}, u32[]{:S(2)}) copy-start(f32[6,2,8,256]{3,2,1,0:T(8,128)} %get-tuple-element.74) | copy-start | bytes 294916
  287.4 5.8 %copy-start.10 = (f32[2048,32]{1,0:T(8,128)S(1)}, f32[2048,32]{1,0:T(8,128)}, u32[]{:S(2)}) copy-start(f32[2048,32]{1,0:T(8,128)} %constant.21.clone) | copy-start | bytes 786436
  (4 other events, 6.4 us)
